TPU v7x, 256 devices: a whole 4x4x8 slice. The times are simulated.
256 devices in a mesh: row: 16 (over x, y), col: 8 (over z_lo, core), layer: 2 (over z_hi).
Axes of the slice: x: 4, y: 4, z: 8 (z_hi: 2, z_lo: 4; z = z_hi * 4 + z_lo), core: 2. Of those that a mesh axis runs over, the one named last changes fastest.
Arguments:
- tasks: bfloat16 [16384, 4096], P(('row', 'col')), may hold values from -0.1875 to 0.1875
- task_owner: int32 [16384, 1], P(('row', 'col')), may hold values from 0 to 127; in each aligned block of 128 rows (0 to 127, 128 to 255, ...) at most 2 rows name the same one
- task_slot: int32 [16384], P(('row', 'col')), may hold values from 0 to 127
- p_pattern: int32 [128, 128], P('row', 'col'), may hold values from 0 to 1, as said below
- c_pattern: int32 [128, 128], P('row', 'col'), may hold values from 0 to 1, as said below
- occupations: float32 [8192], P('row'), may hold values from 0.1 to 0.9
Outputs:
- purified: float32 [8192, 8192], P(('row', 'layer'), 'col')
Inputs may be any that keep to these rules, and one draw needn't show every extreme that they name: `task_owner`: the 128 tasks of one index of row and col name each owner at most 2 times. `task_slot`: a block of the owner's 8 x 16 blocks, row-major. `p_pattern`: 0 or 1; every diagonal block is 1. `c_pattern`: 0 or 1; every diagonal block is 1.
All inputs are finite; a program needn't handle non-finite values.
Results may differ from a plain program's by a relative error of at most 0.025.
Values may be sent and summed in bfloat16 or wider, within the bound.
A program may use at most 64 MiB of HBM per device.

v0:
```python
import jax
import jax.numpy as jnp
from jax import lax
from jax.sharding import PartitionSpec as P

BLK = 64


def expand_blocks(pattern):
    return jnp.repeat(jnp.repeat(pattern.astype(jnp.float32), BLK, axis=0), BLK, axis=1)


def column_units(tile, layers, layer):
    rows, cols = tile.shape
    unit = rows // layers
    split = tile.reshape(rows, cols // (layers * unit), layers, unit)
    picked = lax.dynamic_index_in_dim(split, layer, axis=2, keepdims=False)
    return picked.reshape(rows, cols // layers)


def row_unit(tile, layers, layer):
    unit = tile.shape[0] // layers
    return lax.dynamic_slice_in_dim(tile, layer * unit, unit, 0)


def fold_rows(piece_rows, left_panel):
    return jnp.dot(
        left_panel,
        lax.all_gather(piece_rows, "row", axis=0, tiled=True),
        preferred_element_type=jnp.float32,
    )


def on_device(tasks, task_owner, task_slot, p_pattern, c_pattern, occupations):
    owners = lax.axis_size("row") * lax.axis_size("col")
    task_count = tasks.shape[0]
    capacity = max(2, 2 * task_count // owners)
    block_rows, block_cols = p_pattern.shape
    slots_here = block_rows * block_cols
    owner = task_owner[:, 0]
    same = (owner[:, None] == jnp.arange(owners, dtype=jnp.int32)[None, :]).astype(jnp.int32)
    placed = jnp.sum(jnp.cumsum(same, axis=0) * same, axis=1) - 1
    target = owner * capacity + placed
    send_blocks = jnp.zeros((owners * capacity, BLK * BLK), jnp.bfloat16).at[target].set(tasks)
    send_slots = (
        jnp.full((owners * capacity,), -1.0, jnp.bfloat16)
        .at[target]
        .set(task_slot.astype(jnp.bfloat16))
    )
    got_blocks, got_slots = (
        lax.all_to_all(
            send_blocks.reshape(owners, capacity, BLK * BLK),
            ("row", "col"),
            split_axis=0,
            concat_axis=0,
            tiled=True,
        ),
        lax.all_to_all(
            send_slots.reshape(owners, capacity),
            ("row", "col"),
            split_axis=0,
            concat_axis=0,
            tiled=True,
        ),
    )
    marks = (
        got_slots.reshape(-1).astype(jnp.float32)[:, None]
        == jnp.arange(slots_here, dtype=jnp.float32)[None, :]
    ).astype(jnp.bfloat16)
    summed = lax.dot_general(
        marks,
        got_blocks.reshape(-1, BLK * BLK),
        (((0,), (0,)), ((), ())),
        preferred_element_type=jnp.float32,
    )
    tile_rows = block_rows * BLK
    tile_cols = block_cols * BLK
    assembled = (
        summed.reshape(block_rows, block_cols, BLK, BLK)
        .transpose(0, 2, 1, 3)
        .reshape(tile_rows, tile_cols)
    )
    row_start = lax.axis_index("row") * tile_rows
    col_start = lax.axis_index("col") * tile_cols
    on_diagonal = (row_start + jnp.arange(tile_rows))[:, None] == (
        col_start + jnp.arange(tile_cols)
    )[None, :]
    density = (
        expand_blocks(p_pattern) * assembled + jnp.where(on_diagonal, occupations[:, None], 0.0)
    ).astype(jnp.bfloat16)
    layers = lax.axis_size("layer")
    layer = lax.axis_index("layer")
    left_piece = column_units(density, layers, layer)
    right_piece = row_unit(density, layers, layer)
    left_panel = lax.all_gather(left_piece, "col", axis=1, tiled=True)
    partial_square = fold_rows(right_piece, left_panel)
    square = lax.psum(partial_square.astype(jnp.bfloat16), "layer").astype(jnp.float32)
    square_rows = row_unit(square, layers, layer)
    partial_cube = fold_rows(square_rows.astype(jnp.bfloat16), left_panel)
    cube_rows = row_unit(
        lax.psum(partial_cube.astype(jnp.bfloat16), "layer").astype(jnp.float32), layers, layer
    )
    mask_rows = row_unit(expand_blocks(c_pattern), layers, layer)
    return mask_rows * (3.0 * square_rows - 2.0 * cube_rows)


def solution(mesh):
    return jax.shard_map(
        on_device,
        mesh=mesh,
        in_specs=(
            P(("row", "col"), None),
            P(("row", "col"), None),
            P(("row", "col")),
            P("row", "col"),
            P("row", "col"),
            P("row"),
        ),
        out_specs=P(("row", "layer"), "col"),
        check_vma=False,
    )
```

profile of v0, /device:TPU:8, one launch (start us, length us, event | category | flops | bytes accessed | tf_op | source)
XLA Modules:
  0.0 507.9 jit_solution(2555189373644705348)
XLA Ops:
  6.5 0.7 convert_element_type.47
  7.2 0.7 fusion.12
  7.9 0.2 reduce_window_sum.11
  8.1 0.8 select_reduce_fusion
  8.9 0.7 fusion.13
  9.6 1.3 scatter_custom_fusion
  11.0 0.8 all_to_all.12
  11.8 12.8 %all-to-all-start = ((bf16[128,1,2]{2,1,0:T(2,128)(2,1)}), bf16[128,1,2]{2,1,0:T(2,128)(2,1)S(1)}, u32[]{:S(2)}, u32[]{:S(2)}) async-start(bf16[128,1,2]{2,1,0:T(2,128)(2,1)} %all_to_all.12), calls=%async_computation | async-start | bytes 131072 | tf_op jit(solution)/shard_map/all_to_all | solution.py:58
  24.5 3.4 scatter_custom_fusion.1
  28.0 2.6 reshape.102
  30.6 3.3 all-to-all-done
  33.9 8.6 %all-to-all-start.1 = ((bf16[128,2,4096]{2,1,0:T(2,128)(2,1)}), bf16[128,2,4096]{2,1,0:T(2,128)(2,1)S(1)}, u32[]{:S(2)}, u32[]{:S(2)}) async-start(bf16[128,2,4096]{2,1,0:T(2,128)(2,1)} %reshape.102), calls=%async_computation.1 | async-start | bytes 4194304 | tf_op jit(solution)/shard_map/all_to_all | solution.py:51
  42.5 0.2 all-gather.4.cloned.1.call-start
  42.7 0.1 copy.15
  42.8 0.1 broadcast_in_dim.44
  42.9 0.1 reshape.100
  43.0 0.2 convert_reduce_fusion
  43.2 0.1 reshape.108
  43.3 48.0 %all-to-all-done.1 = bf16[128,2,4096]{2,1,0:T(2,128)(2,1)S(1)} async-done(((bf16[128,2,4096]{2,1,0:T(2,128)(2,1)}), bf16[128,2,4096]{2,1,0:T(2,128)(2,1)S(1)}, u32[]{:S(2)}, u32[]{:S(2)}) %all-to-all-start.1) | async-done | bytes 2097184 | tf_op jit(solution)/shard_map/all_to_all | solution.py:51
  91.3 2.2 reshape.103
  93.5 3.3 copy.17
  96.8 3.2 convolution_bitcast_fusion
  100.0 4.1 reshape.104
  104.1 1.9 constant_dynamic-slice_fusion.2
  106.0 2.4 copy.22
  108.3 0.2 broadcast_in_dim.45
  108.6 1.0 fusion.5
  109.7 0.1 dynamic-slice.2
  109.8 0.1 dynamic-slice.1
  109.9 4.9 reshape.107
  114.7 2.3 constant_dynamic-slice_fusion.1
  117.0 1.6 copy.23
  118.6 1.0 fusion.3
  119.7 44.1 %all-gather.4.cloned.1.call-done = bf16[512,4096]{0,1:T(8,128)(2,1)} async-done(((bf16[512,512]{0,1:T(8,128)(2,1)}), bf16[512,4096]{0,1:T(8,128)(2,1)}) %all-gather.4.cloned.1.call-update) | async-done | bytes 4194320 | tf_op jit(solution)/shard_map/all_gather | solution.py:95
  163.8 84.0 %all-gather.6.cloned.1.call-done = bf16[4096,1024]{0,1:T(8,128)(2,1)} async-done(((bf16[256,1024]{0,1:T(8,128)(2,1)}), bf16[4096,1024]{0,1:T(8,128)(2,1)}) %all-gather.6.cloned.1.call-update) | async-done | bytes 8388624 | tf_op jit(solution)/shard_map/all_gather | solution.py:29
  247.8 10.2 %convolution_convert_fusion.1 = bf16[512,1024]{1,0:T(8,128)(2,1)} fusion(bf16[512,4096]{0,1:T(8,128)(2,1)} %all-gather.4.cloned.1.call-done, bf16[4096,1024]{0,1:T(8,128)(2,1)} %all-gather.6.cloned.1.call-done), kind=kOutput, calls=%fused_computation.4 | convolution fusion | flops 4295491584 | bytes 13631488 | tf_op jit(solution)/shard_map/dot_general | solution.py:27
  258.1 78.1 %all-reduce.3.cloned.1.call-done = bf16[512,1024]{1,0:T(8,128)(2,1)} async-done(((bf16[512,1024]{1,0:T(8,128)(2,1)}), bf16[512,1024]{1,0:T(8,128)(2,1)}) %all-reduce.3.cloned.1.call-update) | async-done | bytes 1048592 | tf_op jit(solution)/shard_map/psum | solution.py:97
  336.2 1.9 convert_convert_fusion
  338.1 0.3 all-reduce.5.cloned.1.call-start
  338.4 72.4 %all-gather.8.cloned.1.call-done = bf16[4096,1024]{1,0:T(8,128)(2,1)} async-done(((bf16[256,1024]{1,0:T(8,128)(2,1)}), bf16[4096,1024]{1,0:T(8,128)(2,1)}) %all-gather.8.cloned.1.call-update) | async-done | bytes 8388624 | tf_op jit(solution)/shard_map/all_gather | solution.py:29
  410.8 10.1 %convolution_convert_fusion = bf16[512,1024]{1,0:T(8,128)(2,1)} fusion(bf16[512,4096]{0,1:T(8,128)(2,1)} %all-gather.4.cloned.1.call-done, bf16[4096,1024]{1,0:T(8,128)(2,1)} %all-gather.8.cloned.1.call-done), kind=kOutput, calls=%fused_computation.3 | convolution fusion | flops 4295491584 | bytes 13631488 | tf_op jit(solution)/shard_map/dot_general | solution.py:27
  421.1 0.1 broadcast_in_dim.42
  421.1 0.1 reshape.98
  421.2 0.3 broadcast_in_dim.43
  421.5 0.1 constant_dynamic-slice_fusion.3
  421.6 0.3 copy.21
  421.9 77.2 %all-reduce.5.cloned.1.call-done = bf16[512,1024]{1,0:T(8,128)(2,1)} async-done(((bf16[512,1024]{1,0:T(8,128)(2,1)}), bf16[512,1024]{1,0:T(8,128)(2,1)}) %all-reduce.5.cloned.1.call-update) | async-done | bytes 1048592 | tf_op jit(solution)/shard_map/psum | solution.py:101
  499.1 2.2 fusion.1
  (24 shorter events, 0.3 us)
Async XLA Ops:
  11.8 22.1 %all-to-all-start = ((bf16[128,1,2]{2,1,0:T(2,128)(2,1)}), bf16[128,1,2]{2,1,0:T(2,128)(2,1)S(1)}, u32[]{:S(2)}, u32[]{:S(2)}) async-start(bf16[128,1,2]{2,1,0:T(2,128)(2,1)} %all_to_all.12), calls=%async_computation | async-start | bytes 131072 | tf_op jit(solution)/shard_map/all_to_all | solution.py:58
  30.6 12.1 %copy-start.2 = (s32[8,16]{1,0:T(8,128)S(1)}, s32[8,16]{1,0:T(8,128)}, u32[]{:S(2)}) copy-start(s32[8,16]{1,0:T(8,128)} %param.9) | copy-start | bytes 1540
  33.9 57.4 %all-to-all-start.1 = ((bf16[128,2,4096]{2,1,0:T(2,128)(2,1)}), bf16[128,2,4096]{2,1,0:T(2,128)(2,1)S(1)}, u32[]{:S(2)}, u32[]{:S(2)}) async-start(bf16[128,2,4096]{2,1,0:T(2,128)(2,1)} %reshape.102), calls=%async_computation.1 | async-start | bytes 4194304 | tf_op jit(solution)/shard_map/all_to_all | solution.py:51
  42.5 121.3 %all-gather.4.cloned.1.call-start = ((), (), s32[]{:S(2)}) async-start(), calls=%async_computation.2 | async-start | bytes 4718592 | tf_op jit(solution)/shard_map/all_gather | solution.py:95
  106.0 2.6 copy-start.1
  109.7 138.2 %all-gather.6.cloned.1.call-start = ((), (), s32[]{:S(2)}) async-start(), calls=%async_computation.3 | async-start | bytes 8912896 | tf_op jit(solution)/shard_map/all_gather | solution.py:29
  119.6 216.6 %all-reduce.3.cloned.1.call-start = ((), (), s32[]{:S(2)}) async-start(), calls=%async_computation.4 | async-start | bytes 2097152 | tf_op jit(solution)/shard_map/psum | solution.py:97
  258.0 152.8 %all-gather.8.cloned.1.call-start = ((), (), s32[]{:S(2)}) async-start(), calls=%async_computation.5 | async-start | bytes 8912896 | tf_op jit(solution)/shard_map/all_gather | solution.py:29
  338.1 82.9 %copy-start.3 = (s32[8,16]{1,0:T(8,128)S(1)}, s32[8,16]{1,0:T(8,128)}, u32[]{:S(2)}) copy-start(s32[8,16]{1,0:T(8,128)} %param.10) | copy-start | bytes 1540
  338.1 161.0 %all-reduce.5.cloned.1.call-start = ((), (), s32[]{:S(2)}) async-start(), calls=%async_computation.6 | async-start | bytes 2097152 | tf_op jit(solution)/shard_map/psum | solution.py:101
  421.5 77.7 %copy-start = (bf16[512,1024]{1,0:T(8,128)(2,1)S(1)}, bf16[512,1024]{1,0:T(8,128)(2,1)}, u32[]{:S(2)}) copy-start(bf16[512,1024]{1,0:T(8,128)(2,1)} %all-reduce.3.cloned.1.call-done) | copy-start | bytes 3145732
Sparse Core Ops, SparseCore 0:
  109.8 53.9 all-gather.3
  166.2 81.5 all-gather.5
  258.1 78.0 all-reduce.2
  338.8 71.9 all-gather.7
  421.1 78.0 all-reduce.4
where the time goes:
time: 510 us; the launch traced here: 508 us
  waiting for transfers between devices  407 us (80%)
  local copies, waits for them, and re-layouts  32.5 us (6%)
  matrix products  23.5 us (5%)
  starting transfers between devices  22 us (4%)
  between operations  13.4 us (3%)
  other arithmetic  9.42 us (2%)
    all_gather x2, waiting for transfers between devices, fold_rows(): lax.all_gather(piece_rows, 'row', axis=0, tiled=True)  156 us
    psum x1, waiting for transfers between devices, on_device(): lax.psum(partial_square.astype(jnp.bfloat16), 'layer').astype(jnp.float32)  78.1 us
    psum x1, waiting for transfers between devices, on_device(): lax.psum(partial_cube.astype(jnp.bfloat16), 'layer').astype(jnp.float32)  77.2 us
    all_to_all x1, waiting for transfers between devices, on_device(): lax.all_to_all(send_blocks.reshape(owners, capacity, BLK * BLK), ('row',...  48 us
    all_gather x1, waiting for transfers between devices, on_device(): left_panel = lax.all_gather(left_piece, 'col', axis=1, tiled=True)  44.1 us
    dot_general x2, matrix products, fold_rows(): jnp.dot(left_panel, lax.all_gather(piece_rows, 'row', axis=0, tiled=True)...  20.3 us
    all_to_all x1, starting transfers between devices, on_device(): lax.all_to_all(send_slots.reshape(owners, capacity), ('row', 'col'), spli...  12.8 us
  transfers between devices with their start and end apart: 7, of which 7 were waited for; matrix products, arithmetic and copies ran while one was open for 3% of the time, Pallas kernels for 0%

commit v1 on v0

v1 whole, which is shorter than its diff:
```python
import functools

import jax
import jax.numpy as jnp
from jax import lax
from jax.experimental import pallas as pl
from jax.experimental.pallas import tpu as pltpu
from jax.sharding import PartitionSpec as P

BLK = 64
HALF = 32
MESH = pl.DeviceIdType.MESH
BF16 = jnp.bfloat16
F32 = jnp.float32


def iota(shape, axis):
    return lax.broadcasted_iota(jnp.int32, shape, axis)


def dot(a, b):
    return jnp.dot(a, b, preferred_element_type=F32)


def pack_kernel(task_ref, owner_col_ref, owner_row_ref, slot_ref, out_ref):
    count = task_ref.shape[0]
    half = lax.axis_index("layer")
    earlier = iota((count, count), 0) < iota((count, count), 1)
    same = (owner_col_ref[...] == owner_row_ref[...]) & earlier
    placed = jnp.sum(same.astype(jnp.int32), axis=0, keepdims=True)
    target = owner_row_ref[...] * 2 + placed
    put = (iota((2 * count, count), 0) == target).astype(BF16)
    lane = iota((256, 128), 0)
    want = iota((256, 128), 1)
    source = (want // HALF) * BLK + half * HALF + want % HALF
    pick = (lane == source).astype(BF16)
    for group in range(task_ref.shape[1] // 256):
        piece = dot(task_ref[:, group * 256 : (group + 1) * 256], pick).astype(BF16)
        out_ref[:, group * 128 : (group + 1) * 128] = dot(put, piece).astype(BF16)
    slot = slot_ref[...]
    order = (slot % 16) * 8 + slot // 16
    marks = jnp.broadcast_to(order + 1, (count, 128)).astype(BF16)
    out_ref[:, 2048:2176] = (dot(put, marks) - 1.0).astype(BF16)


def assemble_kernel(got_ref, pattern_ref, occ_ref, out_ref, rows):
    row_id = lax.axis_index("row") * 512
    col_id = lax.axis_index("col") * 1024 + lax.axis_index("layer") * HALF
    entries = got_ref.shape[0]
    marks = (got_ref[:, 2048:2176].astype(F32) == iota((entries, 128), 1).astype(F32)).astype(BF16)
    spread = (iota((16, 512), 0) == iota((16, 512), 1) // HALF).astype(F32)
    mask = dot(pattern_ref[...].astype(F32), spread)
    column = col_id + (iota((8, 512), 1) // HALF) * BLK + iota((8, 512), 1) % HALF
    first = row_id + iota((8, 512), 0) * BLK
    quarter = iota((8, 128), 1) // HALF
    for quad in range(16):
        summed = lax.dot_general(
            marks,
            got_ref[:, quad * 128 : (quad + 1) * 128],
            (((0,), (0,)), ((), ())),
            preferred_element_type=F32,
        )
        for e in range(4):
            tiles = []
            for t in range(4):
                tile = None
                for f in range(4):
                    block = t * 4 + f
                    value = summed[block * 8 : (block + 1) * 8, :]
                    shift = (f - e) % 4
                    if shift:
                        value = pltpu.roll(value, shift * HALF, 1)
                    tile = value if tile is None else jnp.where(quarter == f, value, tile)
                tiles.append(tile)
            i = quad * 4 + e
            line = jnp.concatenate(tiles, axis=1) * mask
            line = line + jnp.where(first + i == column, occ_ref[:, i : i + 1], 0.0)
            rows[i * 8 : (i + 1) * 8, :] = line
    want = iota((256, 256), 0)
    have = iota((256, 256), 1)
    move = (have == (want % HALF) * 8 + want // HALF).astype(BF16)
    for h in range(2):
        out_ref[h] = dot(move, rows[h * 256 : (h + 1) * 256, :].astype(BF16)).astype(BF16)


def step_kernel(
    d_ref, pattern_ref, out_ref,
    a, b, b2, acc, keep, near, far, near_in, far_in, mixed, swapped,
    local_sem, y_send, y_recv, z_send, z_recv, twin_send, twin_recv,
    x_send, x_recv, r_send, r_recv, swap_send, swap_recv,
):
    row, col, layer = lax.axis_index("row"), lax.axis_index("col"), lax.axis_index("layer")
    x, y = row // 4, row % 4
    core = col % 2
    z = layer * 4 + col // 2

    def device(xx, yy, zz, cc):
        return (xx * 4 + yy, (zz % 4) * 2 + cc, zz // 4)

    def ring(value, step, size):
        return (value + step + size) % size

    twin = device(x, y, z, 1 - core)
    up_y, down_y = device(x, ring(y, 1, 4), z, core), device(x, ring(y, -1, 4), z, core)
    up_x, down_x = device(ring(x, 1, 4), y, z, core), device(ring(x, -1, 4), y, z, core)
    up_z, down_z = device(x, y, ring(z, 1, 8), core), device(x, y, ring(z, -1, 8), core)
    across = device(x, y, ring(z, 4, 8), core)

    barrier = pltpu.get_barrier_semaphore()
    others = [device(x, ring(y, s, 4), z, c) for s in range(1, 4) for c in range(2)]
    others += [twin, up_x, down_x, up_z, down_z, across]
    for other in others:
        pl.semaphore_signal(barrier, inc=1, device_id=other, device_id_type=MESH)
    pl.semaphore_wait(barrier, len(others))

    def remote(src, dst, send, recv, to):
        return pltpu.make_async_remote_copy(
            src_ref=src, dst_ref=dst, send_sem=send, recv_sem=recv, device_id=to, device_id_type=MESH
        )

    y_copies = []
    for p in range(2):
        for c in range(2):
            to_y = 2 * core + p
            mine = jnp.logical_and(to_y == y, core == c)
            src = d_ref.at[c, :, pl.ds(p * 256, 256)]
            dst = a.at[z, c * 4 + y]
            copy = remote(src, dst, y_send.at[p * 2 + c], y_recv.at[y], device(x, to_y, z, c))
            own = pltpu.make_async_copy(src, dst, local_sem.at[0])

            @pl.when(jnp.logical_not(mine))
            def _():
                copy.start()

            @pl.when(mine)
            def _():
                own.start()

            y_copies.append((mine, copy, own))

    def x_first(source, panel, sems):
        up = remote(source, panel.at[:, x], x_send.at[sems], x_recv.at[sems], up_x)
        down = remote(source, panel.at[:, x], x_send.at[sems + 1], x_recv.at[sems + 1], down_x)
        home = pltpu.make_async_copy(source, panel.at[:, x], local_sem.at[1 + sems // 4])
        up.start()
        down.start()
        home.start()
        return up, down, home

    def x_second(panel, sems, first):
        first[0].wait_recv()
        left = ring(x, -1, 4)
        up = remote(panel.at[0, left], panel.at[0, left], x_send.at[sems + 2], x_recv.at[sems + 2], up_x)
        up.start()
        first[1].wait_recv()
        right = ring(x, 1, 4)
        down = remote(panel.at[1, right], panel.at[1, right], x_send.at[sems + 3], x_recv.at[sems + 3], down_x)
        down.start()
        return up, down

    x_one = x_first(d_ref, b, 0)

    for source_y in range(4):
        mine = jnp.logical_and(y == source_y, core == y // 2)
        block = a.at[z, core * 4 + source_y]

        @pl.when(jnp.logical_not(mine))
        def _():
            remote(block, block, y_send.at[0], y_recv.at[source_y], twin).wait_recv()

        @pl.when(mine)
        def _():
            pltpu.make_async_copy(block, block, local_sem.at[0]).wait()

    def part(zz, low, size):
        return a.at[zz, pl.ds(core * 4 + low, size)]

    pending = []

    def z_send_step(step):
        up_block, down_block = ring(z, 1 - step, 8), ring(z, step - 1, 8)
        size = 4 if step < 4 else 2
        ups = part(up_block, 0, size)
        downs = part(down_block, 4 - size, size)
        up = remote(ups, ups, z_send.at[step - 1], z_recv.at[step - 1], up_z)
        down = remote(downs, downs, z_send.at[step + 3], z_recv.at[step + 3], down_z)
        up.start()
        down.start()
        return up, down

    def twin_send_step(index, zz, low, size):
        ref = part(zz, low, size)
        copy = remote(ref, ref, twin_send.at[index], twin_recv.at[index], twin)
        copy.start()
        pending.append(copy)

    def twin_wait(index, zz, low, size):
        ref = a.at[zz, pl.ds((1 - core) * 4 + low, size)]
        remote(ref, ref, twin_send.at[index], twin_recv.at[index], twin).wait_recv()

    def hand_over(step):
        size = 4 if step < 4 else 2
        twin_send_step(2 * step - 1, ring(z, -step, 8), 0, size)
        twin_send_step(2 * step, ring(z, step, 8), 4 - size, size)

    def take_over(step):
        size = 4 if step < 4 else 2
        twin_wait(2 * step - 1, ring(z, -step, 8), 0, size)
        twin_wait(2 * step, ring(z, step, 8), 4 - size, size)

    def product(blocks, right, first):
        pieces = [(zz, right[zz // 4, zz % 4]) for zz in blocks]

        def body(m, carry):
            total = None
            for zz, piece in pieces:
                term = dot(a[zz, m], piece)
                total = term if total is None else total + term
            acc[m] = total if first else acc[m] + total
            return carry

        lax.fori_loop(0, 8, body, 0)

    z_one = z_send_step(1)
    twin_send_step(0, z, 0, 4)
    x_two = x_second(b, 0, x_one)
    for copy in z_one:
        copy.wait_recv()
    z_two = z_send_step(2)
    hand_over(1)
    for copy in x_two:
        copy.wait_recv()
    x_one[2].wait()
    twin_wait(0, z, 0, 4)
    product([z], b, True)
    take_over(1)
    product([ring(z, -1, 8), ring(z, 1, 8)], b, False)
    for copy in z_two:
        copy.wait_recv()
    z_three = z_send_step(3)
    hand_over(2)
    take_over(2)
    product([ring(z, -2, 8), ring(z, 2, 8)], b, False)
    for copy in z_three:
        copy.wait_recv()
    z_four = z_send_step(4)
    hand_over(3)
    take_over(3)
    product([ring(z, -3, 8), ring(z, 3, 8)], b, False)
    for copy in z_four:
        copy.wait_recv()
    hand_over(4)
    take_over(4)
    product([ring(z, 4, 8)], b, False)

    def reduce(index):
        up_t, down_t, far_t = ring(y, 1, 4), ring(y, -1, 4), ring(y, 2, 4)
        base = index * 6

        def send(k, src, dst, to):
            copy = remote(src, dst, r_send.at[base + k], r_recv.at[base + k], to)
            copy.start()
            return copy

        far[index, 0] = acc[far_t].astype(BF16)
        far_up = send(0, far.at[index, 0], far_in.at[index, 0], up_y)
        far[index, 1] = acc[4 + far_t].astype(BF16)
        far_down = send(1, far.at[index, 1], far_in.at[index, 1], down_y)
        near[index, 0, 1] = acc[4 + up_t].astype(BF16)
        up_plain = send(2, near.at[index, 0, 1], near_in.at[index, 0, 1], up_y)
        near[index, 1, 0] = acc[down_t].astype(BF16)
        down_plain = send(3, near.at[index, 1, 0], near_in.at[index, 1, 0], down_y)
        far_up.wait_recv()
        near[index, 0, 0] = (acc[up_t] + far_in[index, 0].astype(F32)).astype(BF16)
        up_sum = send(4, near.at[index, 0, 0], near_in.at[index, 0, 0], up_y)
        far_down.wait_recv()
        near[index, 1, 1] = (acc[4 + down_t] + far_in[index, 1].astype(F32)).astype(BF16)
        down_sum = send(5, near.at[index, 1, 1], near_in.at[index, 1, 1], down_y)
        copies = [far_up, far_down, up_plain, down_plain, up_sum, down_sum]
        for copy in copies[2:]:
            copy.wait_recv()
        for copy in copies:
            copy.wait_send()
        return [
            acc[half * 4 + y] + near_in[index, 0, half].astype(F32) + near_in[index, 1, half].astype(F32)
            for half in range(2)
        ]

    square = reduce(0)
    for half in range(2):
        keep[half] = square[half]
        mixed[half] = square[half].astype(BF16)
    x_three = x_first(mixed, b2, 4)
    x_three[2].wait()
    product([x, x + 4], b2, True)
    x_four = x_second(b2, 4, x_three)
    left, right = ring(x, -1, 4), ring(x, 1, 4)
    product([left, left + 4, right, right + 4], b2, False)
    for copy in x_four:
        copy.wait_recv()
    opposite = ring(x, 2, 4)
    product([opposite, opposite + 4], b2, False)
    for copy in x_three[:2]:
        copy.wait_send()
    cube = reduce(1)
    for half in range(2):
        mixed[half] = (3.0 * keep[half] - 2.0 * cube[half]).astype(BF16)

    swap = remote(
        mixed.at[:, pl.ds((1 - layer) * 128, 128)], swapped, swap_send, swap_recv, across
    )
    swap.start()
    spread = (iota((16, 1024), 0) == iota((16, 1024), 1) // BLK).astype(F32)
    mask_all = dot(pattern_ref[...].astype(F32), spread)
    mask = jnp.where(layer == 0, mask_all[0:4], mask_all[4:8])
    source = iota((256, 256), 0)
    want = iota((256, 256), 1)
    side = jnp.where(source < 128, layer, 1 - layer)
    goes = ((source % 128) // HALF) * BLK + side * HALF + source % HALF
    place = (goes == want).astype(BF16)
    swap.wait_recv()
    for half in range(2):
        own = mixed[half, pl.ds(layer * 128, 128), :]
        other = swapped[half]
        for t in range(4):
            both = jnp.concatenate([own[:, t * 128 : (t + 1) * 128], other[:, t * 128 : (t + 1) * 128]], axis=1)
            full = dot(both, place)
            for blk in range(4):
                out_ref[blk * BLK + half * HALF : blk * BLK + (half + 1) * HALF, t * 256 : (t + 1) * 256] = (
                    full[blk * HALF : (blk + 1) * HALF] * mask[blk : blk + 1, t * 256 : (t + 1) * 256]
                )
    swap.wait_send()

    for mine, copy, own in y_copies:
        @pl.when(jnp.logical_not(mine))
        def _():
            copy.wait_send()

    for copy in (*x_one[:2], *x_two, *x_four, *z_one, *z_two, *z_three, *z_four, *pending):
        copy.wait_send()


VMEM = pl.BlockSpec(memory_space=pltpu.VMEM)


def on_device(tasks, task_owner, task_slot, p_pattern, c_pattern, occupations):
    count = tasks.shape[0]
    packed = pl.pallas_call(
        pack_kernel,
        out_shape=jax.ShapeDtypeStruct((2 * count, 2176), BF16),
        in_specs=[VMEM] * 4,
        out_specs=VMEM,
        compiler_params=pltpu.CompilerParams(vmem_limit_bytes=40 << 20),
        name="pack",
    )(tasks, task_owner, task_owner.reshape(1, count), task_slot.reshape(count, 1))
    got = lax.all_to_all(packed, ("row", "col"), split_axis=0, concat_axis=0, tiled=True)
    density = pl.pallas_call(
        assemble_kernel,
        out_shape=jax.ShapeDtypeStruct((2, 256, 512), BF16),
        in_specs=[VMEM] * 3,
        out_specs=VMEM,
        scratch_shapes=[pltpu.VMEM((512, 512), F32)],
        compiler_params=pltpu.CompilerParams(vmem_limit_bytes=40 << 20),
        name="assemble",
    )(got, p_pattern, occupations.reshape(8, BLK))
    dma = pltpu.SemaphoreType.DMA
    return pl.pallas_call(
        step_kernel,
        out_shape=jax.ShapeDtypeStruct((256, 1024), F32),
        in_specs=[VMEM] * 2,
        out_specs=VMEM,
        scratch_shapes=[
            pltpu.VMEM((8, 8, 256, 256), BF16),
            pltpu.VMEM((2, 4, 256, 512), BF16),
            pltpu.VMEM((2, 4, 256, 512), BF16),
            pltpu.VMEM((8, 256, 512), F32),
            pltpu.VMEM((2, 256, 512), F32),
            pltpu.VMEM((2, 2, 2, 256, 512), BF16),
            pltpu.VMEM((2, 2, 256, 512), BF16),
            pltpu.VMEM((2, 2, 2, 256, 512), BF16),
            pltpu.VMEM((2, 2, 256, 512), BF16),
            pltpu.VMEM((2, 256, 512), BF16),
            pltpu.VMEM((2, 128, 512), BF16),
            dma((3,)),
            dma((4,)),
            dma((4,)),
            dma((8,)),
            dma((8,)),
            dma((9,)),
            dma((9,)),
            dma((8,)),
            dma((8,)),
            dma((12,)),
            dma((12,)),
            dma,
            dma,
        ],
        compiler_params=pltpu.CompilerParams(
            vmem_limit_bytes=56 << 20, collective_id=0, has_side_effects=True
        ),
        name="purify",
    )(density, c_pattern)


def solution(mesh):
    return jax.shard_map(
        on_device,
        mesh=mesh,
        in_specs=(
            P(("row", "col"), None),
            P(("row", "col"), None),
            P(("row", "col")),
            P("row", "col"),
            P("row", "col"),
            P("row"),
        ),
        out_specs=P(("row", "layer"), "col"),
        check_vma=False,
    )
```

time: 510 us -> 194 us (0.38)
  waiting for transfers between devices: 407 us -> 28.4 us
  Pallas kernels: 0 us -> 143 us
  local copies, waits for them, and re-layouts: 32.5 us -> 8.27 us
  matrix products: 23.5 us -> 0 us
  between operations: 13.4 us -> 0.07 us
  other arithmetic: 9.42 us -> 0 us
  starting transfers between devices: 22 us -> 12.9 us
    all_gather x3 -> x0, waiting for transfers between devices: 201 us -> none  [the longest x2 156 us: fold_rows(): lax.all_gather(piece_rows, 'row', axis=0, tiled=True)]
    psum x2 -> x0, waiting for transfers between devices: 155 us -> none  [the longest x1 78.1 us: on_device(): lax.psum(partial_square.astype(jnp.bfloat16), 'layer').astype(jnp.float32)]
    pallas_call x0 -> x3, Pallas kernels: none -> 143 us  [the longest x1 140 us: on_device(): pl.pallas_call(step_kernel, out_shape=jax.ShapeDtypeStruct((256, 1024), F...]
    dot_general x3 -> x0, matrix products: 23.5 us -> none  [the longest x2 20.3 us: fold_rows(): jnp.dot(left_panel, lax.all_gather(piece_rows, 'row', axis=0, tiled=True)...]
    all_to_all x2 -> x1, waiting for transfers between devices: 51.3 us -> 28.4 us  [on_device(): lax.all_to_all(packed, ('row', 'col'), split_axis=0, concat_axis=0, tiled...]
    reshape x6 -> x2, local copies, waits for them, and re-layouts: 14 us -> 0.84 us  [the longest x1 0.76 us: on_device(): task_slot.reshape(count, 1)]
    all_to_all x2 -> x1, starting transfers between devices: 21.4 us -> 12.9 us  [on_device(): lax.all_to_all(packed, ('row', 'col'), split_axis=0, concat_axis=0, tiled...]
    convert_element_type x8 -> x0, other arithmetic: 5.49 us -> none  [the longest x2 2.04 us: on_device(): density = (expand_blocks(p_pattern) * assembled + jnp.where(on_diagonal,...]
  transfers between devices with their start and end apart: 7 -> 1, of which waited for: 7 -> 1; matrix products, arithmetic and copies ran while one was open for 3% -> 0% of each run, Pallas kernels for 0% -> 0%
where the time goes in v1:
time: 194 us; the launch traced here: 192 us
  Pallas kernels  143 us (74%)
  waiting for transfers between devices  28.4 us (15%)
  starting transfers between devices  12.9 us (7%)
  local copies, waits for them, and re-layouts  8.27 us (4%)
    pallas_call x1, Pallas kernels, on_device(): pl.pallas_call(step_kernel, out_shape=jax.ShapeDtypeStruct((256, 1024), F...  140 us
    all_to_all x1, waiting for transfers between devices, on_device(): lax.all_to_all(packed, ('row', 'col'), split_axis=0, concat_axis=0, tiled...  28.4 us
    all_to_all x1, starting transfers between devices, on_device(): lax.all_to_all(packed, ('row', 'col'), split_axis=0, concat_axis=0, tiled...  12.9 us
    unnamed x12, local copies, waits for them, and re-layouts  5.74 us
  transfers between devices with their start and end apart: 1, of which 1 were waited for; matrix products, arithmetic and copies ran while one was open for 0% of the time, Pallas kernels for 0%

profile of v1, /device:TPU:8, one launch (start us, length us, event | category | flops | bytes accessed | tf_op | source)
XLA Modules:
  0.0 192.4 jit_solution(950233518629931895)
XLA Ops:
  0.0 0.8 copy.7.owner_col_ref
  0.8 0.8 copy.8.slot_ref
  1.5 0.0 copy-start.1
  1.5 1.2 copy-done.1
  2.7 0.0 copy-start.3
  2.8 0.7 copy-done.3
  3.4 0.8 pack.1
  4.3 1.3 all_to_all.7
  5.5 0.0 copy-start.4
  5.5 12.9 %all-to-all-start = ((bf16[128,2,2176]{2,1,0:T(2,128)(2,1)}), bf16[128,2,2176]{2,1,0:T(2,128)(2,1)S(1)}, u32[]{:S(2)}, u32[]{:S(2)}) async-start(bf16[128,2,2176]{2,1,0:T(2,128)(2,1)} %all_to_all.7), calls=%async_computation | async-start | bytes 2228224 | tf_op jit(solution)/shard_map/all_to_all | solution.py:356
  18.4 0.0 copy-done.4
  18.4 0.1 reshape.13.occ_ref
  18.5 0.0 copy-start.2
  18.5 28.4 %all-to-all-done = bf16[128,2,2176]{2,1,0:T(2,128)(2,1)S(1)} async-done(((bf16[128,2,2176]{2,1,0:T(2,128)(2,1)}), bf16[128,2,2176]{2,1,0:T(2,128)(2,1)S(1)}, u32[]{:S(2)}, u32[]{:S(2)}) %all-to-all-start) | async-done | bytes 1114144 | tf_op jit(solution)/shard_map/all_to_all | solution.py:356
  46.9 0.4 all_to_all.9.got_ref
  47.3 0.0 copy-done.2
  47.4 1.5 assemble.1.d_ref
  48.9 0.0 copy-start
  48.9 0.8 copy-done
  49.7 140.4 %purify.1 = f32[256,1024]{1,0:T(8,128)} custom-call(bf16[2,256,512]{2,1,0:T(8,128)(2,1)} %copy-done, s32[8,16]{1,0:T(8,128)} %pattern_ref.3), custom_call_target="tpu_custom_call" | custom-call | tf_op jit(solution)/shard_map/purify/pallas_call | solution.py:367
  190.1 2.3 %copy.10 = f32[256,1024]{1,0:T(8,128)} copy(f32[256,1024]{1,0:T(8,128)} %purify.1) | data formatting | bytes 2097152
Async XLA Ops:
  1.5 1.2 copy-start.1
  2.7 0.7 copy-start.3
  5.5 12.9 %copy-start.4 = (f32[512]{0:T(512)S(1)}, f32[512]{0:T(512)}, u32[]{:S(2)}) copy-start(f32[512]{0:T(512)} %param.11) | copy-start | bytes 6148
  5.5 41.4 %all-to-all-start = ((bf16[128,2,2176]{2,1,0:T(2,128)(2,1)}), bf16[128,2,2176]{2,1,0:T(2,128)(2,1)S(1)}, u32[]{:S(2)}, u32[]{:S(2)}) async-start(bf16[128,2,2176]{2,1,0:T(2,128)(2,1)} %all_to_all.7), calls=%async_computation | async-start | bytes 2228224 | tf_op jit(solution)/shard_map/all_to_all | solution.py:356
  18.5 28.8 %copy-start.2 = (s32[8,16]{1,0:T(8,128)S(1)}, s32[8,16]{1,0:T(8,128)}, u32[]{:S(2)}) copy-start(s32[8,16]{1,0:T(8,128)} %pattern_ref.2) | copy-start | bytes 1540
  48.9 0.8 copy-start

commit v2 on v1

v2 whole, which is shorter than its diff:
```python
import functools

import jax
import jax.numpy as jnp
from jax import lax
from jax.experimental import pallas as pl
from jax.experimental.pallas import tpu as pltpu
from jax.sharding import PartitionSpec as P

BLK = 64
HALF = 32
MESH = pl.DeviceIdType.MESH
BF16 = jnp.bfloat16
F32 = jnp.float32


def iota(shape, axis):
    return lax.broadcasted_iota(jnp.int32, shape, axis)


def dot(a, b):
    return jnp.dot(a, b, preferred_element_type=F32)


def pack_kernel(task_ref, owner_col_ref, owner_row_ref, slot_ref, out_ref):
    count = task_ref.shape[0]
    half = lax.axis_index("layer")
    earlier = iota((count, count), 0) < iota((count, count), 1)
    same = (owner_col_ref[...] == owner_row_ref[...]) & earlier
    placed = jnp.sum(same.astype(jnp.int32), axis=0, keepdims=True)
    target = owner_row_ref[...] * 2 + placed
    put = (iota((2 * count, count), 0) == target).astype(BF16)
    lane = iota((256, 128), 0)
    want = iota((256, 128), 1)
    source = (want // HALF) * BLK + half * HALF + want % HALF
    pick = (lane == source).astype(BF16)
    for group in range(task_ref.shape[1] // 256):
        piece = dot(task_ref[:, group * 256 : (group + 1) * 256], pick).astype(BF16)
        out_ref[:, group * 128 : (group + 1) * 128] = dot(put, piece).astype(BF16)
    slot = slot_ref[...]
    order = (slot % 16) * 8 + slot // 16
    marks = jnp.broadcast_to(order + 1, (count, 128)).astype(BF16)
    out_ref[:, 2048:2176] = (dot(put, marks) - 1.0).astype(BF16)


def assemble_kernel(got_ref, pattern_ref, occ_ref, out_ref, rows):
    row_id = lax.axis_index("row") * 512
    col_id = lax.axis_index("col") * 1024 + lax.axis_index("layer") * HALF
    entries = got_ref.shape[0]
    marks = (got_ref[:, 2048:2176].astype(F32) == iota((entries, 128), 1).astype(F32)).astype(BF16)
    spread = (iota((16, 512), 0) == iota((16, 512), 1) // HALF).astype(F32)
    mask = dot(pattern_ref[...].astype(F32), spread)
    column = col_id + (iota((8, 512), 1) // HALF) * BLK + iota((8, 512), 1) % HALF
    first = row_id + iota((8, 512), 0) * BLK
    quarter = iota((8, 128), 1) // HALF
    for quad in range(16):
        summed = lax.dot_general(
            marks,
            got_ref[:, quad * 128 : (quad + 1) * 128],
            (((0,), (0,)), ((), ())),
            preferred_element_type=F32,
        )
        for e in range(4):
            tiles = []
            for t in range(4):
                tile = None
                for f in range(4):
                    block = t * 4 + f
                    value = summed[block * 8 : (block + 1) * 8, :]
                    shift = (f - e) % 4
                    if shift:
                        value = pltpu.roll(value, shift * HALF, 1)
                    tile = value if tile is None else jnp.where(quarter == f, value, tile)
                tiles.append(tile)
            i = quad * 4 + e
            line = jnp.concatenate(tiles, axis=1) * mask
            line = line + jnp.where(first + i == column, occ_ref[:, i : i + 1], 0.0)
            rows[i * 8 : (i + 1) * 8, :] = line
    want = iota((256, 256), 0)
    have = iota((256, 256), 1)
    move = (have == (want % HALF) * 8 + want // HALF).astype(BF16)
    for h in range(2):
        moved = dot(move, rows[h * 256 : (h + 1) * 256, :].astype(BF16)).astype(BF16)
        out_ref[h] = moved.reshape(2, 2, 64, 512)


def step_kernel(
    d_ref, pattern_ref, out_ref,
    a, b, b2, acc, keep, low, near, far, near_in, far_in, result, swapped,
    local_sem, y_send, y_recv, z_send, z_recv, twin_send, twin_recv,
    x_send, x_recv, r_send, r_recv, swap_send, swap_recv,
):
    row, col, layer = lax.axis_index("row"), lax.axis_index("col"), lax.axis_index("layer")
    x, y = row // 4, row % 4
    core = col % 2
    z = layer * 4 + col // 2

    def device(xx, yy, zz, cc):
        return (xx * 4 + yy, (zz % 4) * 2 + cc, zz // 4)

    def ring(value, step, size):
        return (value + step + size) % size

    twin = device(x, y, z, 1 - core)
    up_y, down_y = device(x, ring(y, 1, 4), z, core), device(x, ring(y, -1, 4), z, core)
    up_x, down_x = device(ring(x, 1, 4), y, z, core), device(ring(x, -1, 4), y, z, core)
    up_z, down_z = device(x, y, ring(z, 1, 8), core), device(x, y, ring(z, -1, 8), core)
    across = device(x, y, ring(z, 4, 8), core)

    barrier = pltpu.get_barrier_semaphore()
    others = [device(x, ring(y, s, 4), z, c) for s in range(1, 4) for c in range(2)]
    others += [twin, up_x, down_x, up_z, down_z, across]
    for other in others:
        pl.semaphore_signal(barrier, inc=1, device_id=other, device_id_type=MESH)
    pl.semaphore_wait(barrier, len(others))

    sent = []

    def remote(src, dst, send, recv, to):
        return pltpu.make_async_remote_copy(
            src_ref=src, dst_ref=dst, send_sem=send, recv_sem=recv, device_id=to, device_id_type=MESH
        )

    def launch(src, dst, send, recv, to):
        copy = remote(src, dst, send, recv, to)
        copy.start()
        sent.append(copy)
        return copy

    y_copies = []
    for q in range(4):
        for p in range(2):
            for c in range(2):
                to_y = 2 * core + p
                mine = jnp.logical_and(to_y == y, core == c)
                src = d_ref.at[q // 2, q % 2, c, :, pl.ds(p * 256, 256)]
                dst = a.at[z, q, y, c]
                copy = remote(src, dst, y_send.at[q * 4 + p * 2 + c], y_recv.at[q, y], device(x, to_y, z, c))
                own = pltpu.make_async_copy(src, dst, local_sem.at[q])

                @pl.when(jnp.logical_not(mine))
                def _():
                    copy.start()

                @pl.when(mine)
                def _():
                    own.start()

                y_copies.append((mine, copy))

    def x_first(source, panel, sems, home_sem):
        mine = panel(x)
        up = launch(source, mine, x_send.at[sems], x_recv.at[sems], up_x)
        down = launch(source, mine, x_send.at[sems + 1], x_recv.at[sems + 1], down_x)
        home = pltpu.make_async_copy(source, mine, local_sem.at[home_sem])
        home.start()
        return up, down, home

    x_one = x_first(d_ref, lambda xx: b.at[:, xx], 0, 4)

    def x_second(pieces, sems, first):
        first[0].wait_recv()
        ref = pieces(ring(x, -1, 4), 0)
        up = launch(ref, ref, x_send.at[sems + 2], x_recv.at[sems + 2], up_x)
        first[1].wait_recv()
        ref = pieces(ring(x, 1, 4), 1)
        down = launch(ref, ref, x_send.at[sems + 3], x_recv.at[sems + 3], down_x)
        return up, down

    def y_arrived(q):
        for source_y in range(4):
            mine = jnp.logical_and(y == source_y, core == y // 2)
            block = a.at[z, q, source_y, core]

            @pl.when(jnp.logical_not(mine))
            def _():
                remote(block, block, y_send.at[0], y_recv.at[q, source_y], twin).wait_recv()

            @pl.when(mine)
            def _():
                pltpu.make_async_copy(block, block, local_sem.at[q]).wait()

    z_copies = {}

    def blocks(q, step):
        if step == 4:
            return ((ring(z, -4, 8), 0, 2), (ring(z, 4, 8), 2, 2))
        return ((ring(z, -step, 8), 0, 4), (ring(z, step, 8), 0, 4))

    def z_issue(q, step):
        (up_block, _, _), (down_block, _, _) = blocks(q, step - 1)
        size = 4 if step < 4 else 2
        index = q * 8 + (step - 1) * 2
        ref = a.at[up_block, q, pl.ds(0, size), core]
        up = launch(ref, ref, z_send.at[index], z_recv.at[index], up_z)
        ref = a.at[down_block, q, pl.ds(4 - size, size), core]
        down = launch(ref, ref, z_send.at[index + 1], z_recv.at[index + 1], down_z)
        z_copies[q, step] = (up, down)

    def twin_refs(q, step, side):
        if step == 0:
            return [(q * 9, a.at[z, q, :, side])]
        return [
            (q * 9 + step * 2 - 1 + k, a.at[block, q, pl.ds(low_y, size), side])
            for k, (block, low_y, size) in enumerate(blocks(q, step))
        ]

    def hand_over(q, step):
        for index, ref in twin_refs(q, step, core):
            launch(ref, ref, twin_send.at[index], twin_recv.at[index], twin)

    def z_arrived(q, step):
        for copy in z_copies[q, step]:
            copy.wait_recv()
        hand_over(q, step)

    def product(q, parts, first):
        def body(m, carry):
            total = None
            for zz, piece in parts:
                left = a[zz, q, pl.ds(2 * m, 2)].reshape(256, 256)
                term = dot(left, piece[...].reshape(256, 512))
                total = term if total is None else total + term
            total = total.reshape(2, 2, 64, 512)
            at = pl.ds(2 * m, 2)
            acc[q, at] = total if first else acc[q, at] + total
            return carry

        lax.fori_loop(0, 2, body, 0)

    r_copies = {}
    up_t, down_t, far_t = ring(y, 1, 4), ring(y, -1, 4), ring(y, 2, 4)

    def reduce_issue(n, k, q):
        base = (n * 4 + k) * 6

        def send(j, src, dst, to):
            r_copies[n, k, j] = launch(src, dst, r_send.at[base + j], r_recv.at[base + j], to)

        for side, to in ((0, up_y), (1, down_y)):
            far[n, k, side] = acc[q, far_t, side].astype(BF16)
            send(side, far.at[n, k, side], far_in.at[n, k, side], to)
        for side, t, to in ((0, up_t, up_y), (1, down_t, down_y)):
            near[n, k, side, 1 - side] = acc[q, t, 1 - side].astype(BF16)
            send(2 + side, near.at[n, k, side, 1 - side], near_in.at[n, k, side, 1 - side], to)

    def reduce_pass(n, k, q):
        base = (n * 4 + k) * 6
        for side, t, to in ((0, up_t, up_y), (1, down_t, down_y)):
            r_copies[n, k, side].wait_recv()
            near[n, k, side, side] = (acc[q, t, side] + far_in[n, k, side].astype(F32)).astype(BF16)
            r_copies[n, k, 4 + side] = launch(
                near.at[n, k, side, side], near_in.at[n, k, side, side],
                r_send.at[base + 4 + side], r_recv.at[base + 4 + side], to,
            )

    def reduce_end(n, k, q):
        for j in range(2, 6):
            r_copies[n, k, j].wait_recv()
        return acc[q, y] + near_in[n, k, 0].astype(F32) + near_in[n, k, 1].astype(F32)

    x_copies = {}

    def gather_issue(q):
        value = reduce_end(0, q, q)
        keep[q] = value
        low[q] = value.astype(BF16)
        x_copies[q] = x_first(low.at[q], lambda xx: b2.at[q // 2, xx, q % 2], 4 + 4 * q, 5 + q)

    def gather_pass(q):
        x_copies[q] += x_second(lambda xx, s: b2.at[q // 2, xx, q % 2, s], 4 + 4 * q, x_copies[q])

    def gather_end(q):
        x_copies[q][2].wait()
        for copy in x_copies[q][3:]:
            copy.wait_recv()

    def all_arrived(q):
        for step in range(5):
            for index, ref in twin_refs(q, step, 1 - core):
                remote(ref, ref, twin_send.at[index], twin_recv.at[index], twin).wait_recv()

    def square(q):
        all_arrived(q)
        product(q, [(zz, b.at[zz // 4, zz % 4]) for zz in range(8)], True)
        reduce_issue(0, q, q)

    for q in range(4):
        y_arrived(q)
        hand_over(q, 0)
        if q < 2:
            z_issue(q, 1)
    z_arrived(0, 1)
    z_issue(0, 2)
    z_arrived(1, 1)
    z_issue(1, 2)
    z_arrived(0, 2)
    z_issue(0, 3)
    z_arrived(1, 2)
    z_issue(1, 3)
    x_two = x_second(lambda xx, s: b.at[s, xx], 0, x_one)
    z_arrived(0, 3)
    z_issue(0, 4)
    z_arrived(1, 3)
    z_issue(2, 1)
    z_arrived(0, 4)
    z_issue(1, 4)
    for copy in x_two:
        copy.wait_recv()
    x_one[2].wait()
    square(0)
    z_arrived(2, 1)
    z_issue(3, 1)
    z_arrived(1, 4)
    z_issue(2, 2)
    square(1)
    reduce_pass(0, 0, 0)
    z_arrived(3, 1)
    z_issue(3, 2)
    gather_issue(0)
    reduce_pass(0, 1, 1)
    z_arrived(2, 2)
    z_issue(2, 3)
    gather_issue(1)
    gather_pass(0)
    z_arrived(3, 2)
    z_issue(3, 3)
    gather_pass(1)
    z_arrived(2, 3)
    z_issue(2, 4)
    gather_end(0)
    gather_end(1)
    z_arrived(3, 3)
    z_issue(3, 4)
    z_arrived(2, 4)
    square(2)
    z_arrived(3, 4)
    square(3)
    reduce_pass(0, 2, 2)
    reduce_pass(0, 3, 3)
    for q in range(2):
        product(q, [(zz, b2.at[0, zz]) for zz in range(4)], True)
    gather_issue(2)
    gather_issue(3)
    for q in range(2, 4):
        product(q, [(zz, b2.at[0, zz]) for zz in range(4)], True)
    gather_pass(2)
    gather_pass(3)
    gather_end(2)
    gather_end(3)
    order = [1 - layer, 3 - layer, layer, 2 + layer]
    for k, q in enumerate(order):
        product(q, [(4 + zz, b2.at[1, zz]) for zz in range(4)], False)
        reduce_issue(1, k, q)
    swaps = []
    spread = (iota((16, 1024), 0) == iota((16, 1024), 1) // BLK).astype(F32)
    mask_all = dot(pattern_ref[...].astype(F32), spread)
    mask = jnp.where(layer == 0, mask_all[0:4], mask_all[4:8])
    source = iota((256, 256), 0)
    want = iota((256, 256), 1)
    side = jnp.where(source < 128, layer, 1 - layer)
    goes = ((source % 128) // HALF) * BLK + side * HALF + source % HALF
    place = (goes == want).astype(BF16)

    def finish(k):
        q = order[k]
        result[k] = (3.0 * keep[q] - 2.0 * reduce_end(1, k, q)).astype(BF16)
        if k < 2:
            swaps.append(launch(result.at[k], swapped.at[k], swap_send.at[k], swap_recv.at[k], across))
            return
        half = k - 2
        swaps[half].wait_recv()
        own = result[k].reshape(128, 512)
        other = swapped[half].reshape(128, 512)
        for t in range(4):
            both = jnp.concatenate([own[:, t * 128 : (t + 1) * 128], other[:, t * 128 : (t + 1) * 128]], axis=1)
            full = dot(both, place)
            for blk in range(4):
                out_ref[blk * BLK + half * HALF : blk * BLK + (half + 1) * HALF, t * 256 : (t + 1) * 256] = (
                    full[blk * HALF : (blk + 1) * HALF] * mask[blk : blk + 1, t * 256 : (t + 1) * 256]
                )

    for k, q in enumerate(order):
        reduce_pass(1, k, q)
        if k >= 1:
            finish(k - 1)
    finish(3)

    for mine, copy in y_copies:
        @pl.when(jnp.logical_not(mine))
        def _():
            copy.wait_send()

    for copy in sent:
        copy.wait_send()


VMEM = pl.BlockSpec(memory_space=pltpu.VMEM)


def on_device(tasks, task_owner, task_slot, p_pattern, c_pattern, occupations):
    count = tasks.shape[0]
    packed = pl.pallas_call(
        pack_kernel,
        out_shape=jax.ShapeDtypeStruct((2 * count, 2176), BF16),
        in_specs=[VMEM] * 4,
        out_specs=VMEM,
        compiler_params=pltpu.CompilerParams(vmem_limit_bytes=40 << 20),
        name="pack",
    )(tasks, task_owner, task_owner.reshape(1, count), task_slot.reshape(count, 1))
    got = lax.all_to_all(packed, ("row", "col"), split_axis=0, concat_axis=0, tiled=True)
    density = pl.pallas_call(
        assemble_kernel,
        out_shape=jax.ShapeDtypeStruct((2, 2, 2, 64, 512), BF16),
        in_specs=[VMEM] * 3,
        out_specs=VMEM,
        scratch_shapes=[pltpu.VMEM((512, 512), F32)],
        compiler_params=pltpu.CompilerParams(vmem_limit_bytes=40 << 20),
        name="assemble",
    )(got, p_pattern, occupations.reshape(8, BLK))
    dma = pltpu.SemaphoreType.DMA
    return pl.pallas_call(
        step_kernel,
        out_shape=jax.ShapeDtypeStruct((256, 1024), F32),
        in_specs=[VMEM] * 2,
        out_specs=VMEM,
        scratch_shapes=[
            pltpu.VMEM((8, 4, 4, 2, 64, 256), BF16),
            pltpu.VMEM((2, 4, 2, 2, 64, 512), BF16),
            pltpu.VMEM((2, 4, 2, 2, 64, 512), BF16),
            pltpu.VMEM((4, 4, 2, 64, 512), F32),
            pltpu.VMEM((4, 2, 64, 512), F32),
            pltpu.VMEM((4, 2, 64, 512), BF16),
            pltpu.VMEM((2, 4, 2, 2, 64, 512), BF16),
            pltpu.VMEM((2, 4, 2, 64, 512), BF16),
            pltpu.VMEM((2, 4, 2, 2, 64, 512), BF16),
            pltpu.VMEM((2, 4, 2, 64, 512), BF16),
            pltpu.VMEM((4, 2, 64, 512), BF16),
            pltpu.VMEM((2, 2, 64, 512), BF16),
            dma((9,)),
            dma((16,)),
            dma((4, 4)),
            dma((32,)),
            dma((32,)),
            dma((36,)),
            dma((36,)),
            dma((20,)),
            dma((20,)),
            dma((48,)),
            dma((48,)),
            dma((2,)),
            dma((2,)),
        ],
        compiler_params=pltpu.CompilerParams(
            vmem_limit_bytes=56 << 20, collective_id=0, has_side_effects=True
        ),
        name="purify",
    )(density, c_pattern)


def solution(mesh):
    return jax.shard_map(
        on_device,
        mesh=mesh,
        in_specs=(
            P(("row", "col"), None),
            P(("row", "col"), None),
            P(("row", "col")),
            P("row", "col"),
            P("row", "col"),
            P("row"),
        ),
        out_specs=P(("row", "layer"), "col"),
        check_vma=False,
    )
```

time: 194 us -> 169 us (0.87)
  Pallas kernels: 143 us -> 120 us
    pallas_call x1, Pallas kernels: 140 us -> 117 us  [on_device(): pl.pallas_call(step_kernel, out_shape=jax.ShapeDtypeStruct((256, 1024), F...]
where the time goes in v2:
time: 169 us
  Pallas kernels  120 us (71%)
  waiting for transfers between devices  28.4 us (17%)
  starting transfers between devices  12.9 us (8%)
  local copies, waits for them, and re-layouts  8.27 us (5%)
    pallas_call x1, Pallas kernels, on_device(): pl.pallas_call(step_kernel, out_shape=jax.ShapeDtypeStruct((256, 1024), F...  117 us
    all_to_all x1, waiting for transfers between devices, on_device(): lax.all_to_all(packed, ('row', 'col'), split_axis=0, concat_axis=0, tiled...  28.4 us
    all_to_all x1, starting transfers between devices, on_device(): lax.all_to_all(packed, ('row', 'col'), split_axis=0, concat_axis=0, tiled...  12.9 us
    unnamed x12, local copies, waits for them, and re-layouts  5.74 us
  transfers between devices with their start and end apart: 1, of which 1 were waited for; matrix products, arithmetic and copies ran while one was open for 0% of the time, Pallas kernels for 0%

profile of v2, /device:TPU:8, one launch (start us, length us, event | category | flops | bytes accessed | tf_op | source)
XLA Modules:
  0.0 169.2 jit_solution(13107525313138014152)
XLA Ops:
  0.0 0.8 copy.7.owner_col_ref
  0.8 0.8 copy.8.slot_ref
  1.5 0.0 copy-start.1
  1.5 1.2 copy-done.1
  2.7 0.0 copy-start.3
  2.8 0.7 copy-done.3
  3.4 0.8 pack.1
  4.3 1.3 all_to_all.7
  5.5 0.0 copy-start.4
  5.5 12.9 %all-to-all-start = ((bf16[128,2,2176]{2,1,0:T(2,128)(2,1)}), bf16[128,2,2176]{2,1,0:T(2,128)(2,1)S(1)}, u32[]{:S(2)}, u32[]{:S(2)}) async-start(bf16[128,2,2176]{2,1,0:T(2,128)(2,1)} %all_to_all.7), calls=%async_computation | async-start | bytes 2228224 | tf_op jit(solution)/shard_map/all_to_all | solution.py:411
  18.4 0.0 copy-done.4
  18.4 0.1 reshape.13.occ_ref
  18.5 0.0 copy-start.2
  18.5 28.4 %all-to-all-done = bf16[128,2,2176]{2,1,0:T(2,128)(2,1)S(1)} async-done(((bf16[128,2,2176]{2,1,0:T(2,128)(2,1)}), bf16[128,2,2176]{2,1,0:T(2,128)(2,1)S(1)}, u32[]{:S(2)}, u32[]{:S(2)}) %all-to-all-start) | async-done | bytes 1114144 | tf_op jit(solution)/shard_map/all_to_all | solution.py:411
  46.9 0.4 all_to_all.9.got_ref
  47.3 0.0 copy-done.2
  47.4 1.5 assemble.1.d_ref
  48.9 0.0 copy-start
  48.9 0.8 copy-done
  49.7 117.2 %purify.1 = f32[256,1024]{1,0:T(8,128)} custom-call(bf16[2,2,2,64,512]{4,3,2,1,0:T(8,128)(2,1)} %copy-done, s32[8,16]{1,0:T(8,128)} %pattern_ref.3), custom_call_target="tpu_custom_call" | custom-call | tf_op jit(solution)/shard_map/purify/pallas_call | solution.py:422
  166.9 2.3 %copy.10 = f32[256,1024]{1,0:T(8,128)} copy(f32[256,1024]{1,0:T(8,128)} %purify.1) | data formatting | bytes 2097152
Async XLA Ops:
  1.5 1.2 copy-start.1
  2.7 0.7 copy-start.3
  5.5 12.9 %copy-start.4 = (f32[512]{0:T(512)S(1)}, f32[512]{0:T(512)}, u32[]{:S(2)}) copy-start(f32[512]{0:T(512)} %param.11) | copy-start | bytes 6148
  5.5 41.4 %all-to-all-start = ((bf16[128,2,2176]{2,1,0:T(2,128)(2,1)}), bf16[128,2,2176]{2,1,0:T(2,128)(2,1)S(1)}, u32[]{:S(2)}, u32[]{:S(2)}) async-start(bf16[128,2,2176]{2,1,0:T(2,128)(2,1)} %all_to_all.7), calls=%async_computation | async-start | bytes 2228224 | tf_op jit(solution)/shard_map/all_to_all | solution.py:411
  18.5 28.8 %copy-start.2 = (s32[8,16]{1,0:T(8,128)S(1)}, s32[8,16]{1,0:T(8,128)}, u32[]{:S(2)}) copy-start(s32[8,16]{1,0:T(8,128)} %pattern_ref.2) | copy-start | bytes 1540
  48.9 0.8 copy-start

commit v3 on v2

--- a/solution.py
+++ b/solution.py
@@ -22,44 +22,63 @@
     return jnp.dot(a, b, preferred_element_type=F32)
 
 
-def pack_kernel(task_ref, owner_col_ref, owner_row_ref, slot_ref, out_ref):
+UNITS = ((0, 0, 2), (1, 2, 2), (-1, 4, 2), (2, 6, 1), (-2, 7, 1))
+
+
+def z_shift(unit):
+    near_by = jnp.where(unit < 2, 0, jnp.where(unit < 4, 1, -1))
+    return jnp.where(unit == 6, 2, jnp.where(unit == 7, -2, near_by))
+
+
+def pack(task_ref, owner_ref, slot_ref, z, wide, packed, info):
     count = task_ref.shape[0]
-    half = lax.axis_index("layer")
+    owner = owner_ref[...]
+    column = jnp.transpose(jnp.broadcast_to(owner.astype(F32), (count, count))).astype(jnp.int32)
     earlier = iota((count, count), 0) < iota((count, count), 1)
-    same = (owner_col_ref[...] == owner_row_ref[...]) & earlier
-    placed = jnp.sum(same.astype(jnp.int32), axis=0, keepdims=True)
-    target = owner_row_ref[...] * 2 + placed
-    put = (iota((2 * count, count), 0) == target).astype(BF16)
-    lane = iota((256, 128), 0)
-    want = iota((256, 128), 1)
-    source = (want // HALF) * BLK + half * HALF + want % HALF
+    placed = jnp.sum(jnp.logical_and(column == owner, earlier).astype(jnp.int32), axis=0, keepdims=True)
+    line = iota((256, count), 0)
+    unit = line % 8
+    there = (z + z_shift(unit) + 8) % 8
+    wanted = (((line // 8) % 4) * 4 + (line // 32) % 4) * 8 + (there % 4) * 2 + line // 128
+    put = jnp.logical_and(owner == wanted, placed == unit % 2)
+    halves = jnp.concatenate(
+        [jnp.logical_and(put, there // 4 == h).astype(F32) for h in range(2)], axis=1
+    ).astype(BF16)
+    lane = iota((256, 256), 0)
+    goes = iota((256, 256), 1)
+    source = ((goes % 128) // HALF) * BLK + (goes // 128) * HALF + goes % HALF
     pick = (lane == source).astype(BF16)
-    for group in range(task_ref.shape[1] // 256):
-        piece = dot(task_ref[:, group * 256 : (group + 1) * 256], pick).astype(BF16)
-        out_ref[:, group * 128 : (group + 1) * 128] = dot(put, piece).astype(BF16)
+    for p in range(16):
+        piece = dot(task_ref[:, p * 256 : (p + 1) * 256], pick).astype(BF16)
+        both = jnp.concatenate([piece[:, :128], piece[:, 128:]], axis=0)
+        wide[pl.ds(p, 256, stride=16), :] = dot(halves, both)
+    for part in range(16):
+        value = wide[part * 256 : (part + 1) * 256, :].astype(BF16)
+        packed[part // 8, (part % 8) * 2 : (part % 8) * 2 + 2] = value.reshape(2, 8, 16, 128)
     slot = slot_ref[...]
-    order = (slot % 16) * 8 + slot // 16
-    marks = jnp.broadcast_to(order + 1, (count, 128)).astype(BF16)
-    out_ref[:, 2048:2176] = (dot(put, marks) - 1.0).astype(BF16)
-
-
-def assemble_kernel(got_ref, pattern_ref, occ_ref, out_ref, rows):
-    row_id = lax.axis_index("row") * 512
-    col_id = lax.axis_index("col") * 1024 + lax.axis_index("layer") * HALF
-    entries = got_ref.shape[0]
-    marks = (got_ref[:, 2048:2176].astype(F32) == iota((entries, 128), 1).astype(F32)).astype(BF16)
+    order = (slot % 16) * 8 + slot // 16 + 1
+    mark = jnp.sum(jnp.where(put, order, 0).astype(F32), axis=1, keepdims=True)
+    at = iota((256, 128), 1) == iota((256, 128), 0) // 8
+    rows = (iota((8, 256), 0) == iota((8, 256), 1) % 8).astype(BF16)
+    info[0] = dot(rows, jnp.where(at, mark, 0.0).astype(BF16)) - 1.0
+
+
+def assemble(got, info, lane, row_id, col_id, pattern_ref, occ_ref, wide, rows, out_ref):
+    tiles = [info[k].reshape(128, 128) for k in range(2)]
+    tiles = jnp.concatenate(tiles, axis=0)
+    slot = jnp.sum(jnp.where(iota((256, 128), 1) == lane, tiles, 0.0), axis=1, keepdims=True)
+    marks = jnp.where(slot == iota((256, 128), 1).astype(F32), 1.0, 0.0)
+    marks = jnp.transpose(marks).astype(BF16)
+    for part in range(16):
+        value = got[part // 8, (part % 8) * 2 : (part % 8) * 2 + 2]
+        wide[part * 256 : (part + 1) * 256, :] = value.reshape(256, 128).astype(F32)
     spread = (iota((16, 512), 0) == iota((16, 512), 1) // HALF).astype(F32)
     mask = dot(pattern_ref[...].astype(F32), spread)
     column = col_id + (iota((8, 512), 1) // HALF) * BLK + iota((8, 512), 1) % HALF
     first = row_id + iota((8, 512), 0) * BLK
     quarter = iota((8, 128), 1) // HALF
     for quad in range(16):
-        summed = lax.dot_general(
-            marks,
-            got_ref[:, quad * 128 : (quad + 1) * 128],
-            (((0,), (0,)), ((), ())),
-            preferred_element_type=F32,
-        )
+        summed = dot(marks, wide[pl.ds(quad, 256, stride=16), :].astype(BF16))
         for e in range(4):
             tiles = []
             for t in range(4):
@@ -85,8 +104,9 @@
 
 
 def step_kernel(
-    d_ref, pattern_ref, out_ref,
-    a, b, b2, acc, keep, low, near, far, near_in, far_in, result, swapped,
+    task_ref, owner_ref, slot_ref, p_pattern_ref, occ_ref, pattern_ref, out_ref,
+    wide, packed, by_z, twin_in, by_xy, got, info, info_z, info_xy, rows, d_ref,
+    t_local, t_send, t_recv, a, b, b2, acc, keep, low, near, far, near_in, far_in, result, swapped,
     local_sem, y_send, y_recv, z_send, z_recv, twin_send, twin_recv,
     x_send, x_recv, r_send, r_recv, swap_send, swap_recv,
 ):
@@ -108,10 +128,14 @@
     across = device(x, y, ring(z, 4, 8), core)
 
     barrier = pltpu.get_barrier_semaphore()
-    others = [device(x, ring(y, s, 4), z, c) for s in range(1, 4) for c in range(2)]
-    others += [twin, up_x, down_x, up_z, down_z, across]
+    others = [device(x, ring(y, s, 4), z, 1 - core) for s in range(1, 4)]
+    spot = y * 4 + x
+    plane = [(spot + s) % 16 for s in range(1, 16)]
+    others += [device(at % 4, at // 4, z, core) for at in plane]
+    others += [twin, across] + [device(x, y, ring(z, s, 8), core) for s in (1, -1, 2, -2)]
     for other in others:
         pl.semaphore_signal(barrier, inc=1, device_id=other, device_id_type=MESH)
+    pack(task_ref, owner_ref, slot_ref, z, wide, packed, info)
     pl.semaphore_wait(barrier, len(others))
 
     sent = []
@@ -126,6 +150,68 @@
         copy.start()
         sent.append(copy)
         return copy
+
+    def home(src, dst, index):
+        copy = pltpu.make_async_copy(src, dst, t_local.at[index])
+        copy.start()
+        return copy
+
+    def over_z(source, target, base, own):
+        copies = []
+        for index, (shift, low_unit, size) in enumerate(UNITS[1:]):
+            units = pl.ds(low_unit, size)
+            to = device(x, y, ring(z, shift, 8), core)
+            at = base + index
+            copies.append(launch(source.at[:, units], target.at[:, units], t_send.at[at], t_recv.at[at], to))
+        return copies, home(source.at[:, pl.ds(0, 2)], target.at[:, pl.ds(0, 2)], own)
+
+    def over_plane(source, target, recv, base, own):
+        for index, at in enumerate(plane):
+            to = device(at % 4, at // 4, z, core)
+            launch(source(at), target.at[spot], t_send.at[base + index], t_recv.at[recv], to)
+        copy = home(source(spot), target.at[spot], own)
+        several = target.at[pl.ds(0, 15)]
+
+        def arrived():
+            remote(several, several, t_send.at[0], t_recv.at[recv], twin).wait_recv()
+            copy.wait()
+
+        return arrived
+
+    info_copies = []
+    for index, (shift, _, _) in enumerate(UNITS[1:]):
+        to = device(x, y, ring(z, shift, 8), core)
+        info_copies.append(launch(info.at[0], info_z.at[index], t_send.at[index], t_recv.at[index], to))
+    to_twin = launch(packed.at[1 - core], twin_in, t_send.at[4], t_recv.at[4], twin)
+    z_tasks, z_home = over_z(packed.at[core], by_z, 5, 0)
+    to_twin.wait_recv()
+    plane_b = over_plane(lambda at: twin_in.at[at], by_xy, 13, 13, 1)
+    for copy in info_copies:
+        copy.wait_recv()
+    unit = iota((8, 128), 0)
+    merged = info[0]
+    for index, (_, low_unit, size) in enumerate(UNITS[1:]):
+        fits = jnp.logical_and(unit >= low_unit, unit < low_unit + size)
+        merged = jnp.where(fits, info_z[index], merged)
+    info[1] = merged
+    plane_i = over_plane(lambda at: info.at[1], info_xy.at[0], 14, 28, 2)
+    for copy in z_tasks:
+        copy.wait_recv()
+    z_home.wait()
+    plane_a = over_plane(lambda at: by_z.at[at], got.at[0], 15, 43, 3)
+    plane_b()
+    z_more, z_more_home = over_z(by_xy, got.at[1], 9, 4)
+    plane_i()
+    twin_info = launch(info_xy.at[0], info_xy.at[1], t_send.at[58], t_recv.at[16], twin)
+    plane_a()
+    twin_info.wait_recv()
+    for copy in z_more:
+        copy.wait_recv()
+    z_more_home.wait()
+    assemble(
+        got, info_xy, core * 16 + spot, row * 512, col * 1024 + layer * HALF,
+        p_pattern_ref, occ_ref, wide, rows, d_ref,
+    )
 
     y_copies = []
     for q in range(4):
@@ -399,32 +485,28 @@
 
 
 def on_device(tasks, task_owner, task_slot, p_pattern, c_pattern, occupations):
+    dma = pltpu.SemaphoreType.DMA
     count = tasks.shape[0]
-    packed = pl.pallas_call(
-        pack_kernel,
-        out_shape=jax.ShapeDtypeStruct((2 * count, 2176), BF16),
-        in_specs=[VMEM] * 4,
-        out_specs=VMEM,
-        compiler_params=pltpu.CompilerParams(vmem_limit_bytes=40 << 20),
-        name="pack",
-    )(tasks, task_owner, task_owner.reshape(1, count), task_slot.reshape(count, 1))
-    got = lax.all_to_all(packed, ("row", "col"), split_axis=0, concat_axis=0, tiled=True)
-    density = pl.pallas_call(
-        assemble_kernel,
-        out_shape=jax.ShapeDtypeStruct((2, 2, 2, 64, 512), BF16),
-        in_specs=[VMEM] * 3,
-        out_specs=VMEM,
-        scratch_shapes=[pltpu.VMEM((512, 512), F32)],
-        compiler_params=pltpu.CompilerParams(vmem_limit_bytes=40 << 20),
-        name="assemble",
-    )(got, p_pattern, occupations.reshape(8, BLK))
-    dma = pltpu.SemaphoreType.DMA
     return pl.pallas_call(
         step_kernel,
         out_shape=jax.ShapeDtypeStruct((256, 1024), F32),
-        in_specs=[VMEM] * 2,
+        in_specs=[VMEM] * 6,
         out_specs=VMEM,
         scratch_shapes=[
+            pltpu.VMEM((4096, 128), F32),
+            pltpu.VMEM((2, 16, 8, 16, 128), BF16),
+            pltpu.VMEM((16, 8, 16, 128), BF16),
+            pltpu.VMEM((16, 8, 16, 128), BF16),
+            pltpu.VMEM((16, 8, 16, 128), BF16),
+            pltpu.VMEM((2, 16, 8, 16, 128), BF16),
+            pltpu.VMEM((2, 8, 128), F32),
+            pltpu.VMEM((4, 8, 128), F32),
+            pltpu.VMEM((2, 16, 8, 128), F32),
+            pltpu.VMEM((512, 512), F32),
+            pltpu.VMEM((2, 2, 2, 64, 512), BF16),
+            dma((5,)),
+            dma((59,)),
+            dma((17,)),
             pltpu.VMEM((8, 4, 4, 2, 64, 256), BF16),
             pltpu.VMEM((2, 4, 2, 2, 64, 512), BF16),
             pltpu.VMEM((2, 4, 2, 2, 64, 512), BF16),
@@ -455,7 +537,10 @@
             vmem_limit_bytes=56 << 20, collective_id=0, has_side_effects=True
         ),
         name="purify",
-    )(density, c_pattern)
+    )(
+        tasks, task_owner.reshape(1, count), task_slot.reshape(1, count), p_pattern,
+        occupations.reshape(8, BLK), c_pattern,
+    )
 
 
 def solution(mesh):

time: 169 us -> 150 us (0.89); the launches traced: 169 us -> 148 us
  waiting for transfers between devices: 28.4 us -> 0 us
  Pallas kernels: 120 us -> 144 us
  starting transfers between devices: 12.9 us -> 0 us
  local copies, waits for them, and re-layouts: 8.27 us -> 3.65 us
    all_to_all x1 -> x0, waiting for transfers between devices: 28.4 us -> none  [on_device(): lax.all_to_all(packed, ('row', 'col'), split_axis=0, concat_axis=0, tiled...]
    pallas_call x1, Pallas kernels: 117 us -> 144 us  [on_device(): pl.pallas_call(step_kernel, out_shape=jax.ShapeDtypeStruct((256, 1024), F...]
    all_to_all x1 -> x0, starting transfers between devices: 12.9 us -> none  [on_device(): lax.all_to_all(packed, ('row', 'col'), split_axis=0, concat_axis=0, tiled...]
    unnamed x12 -> x3, local copies, waits for them, and re-layouts: 5.74 us -> 2.99 us
    pallas_call x2 -> x0, Pallas kernels: 2.35 us -> none  [the longest x1 1.5 us: on_device(): pl.pallas_call(assemble_kernel, out_shape=jax.ShapeDtypeStruct((2, 2, 2,...]
    all_to_all x2 -> x0, local copies, waits for them, and re-layouts: 1.69 us -> none  [on_device(): lax.all_to_all(packed, ('row', 'col'), split_axis=0, concat_axis=0, tiled...]
  transfers between devices with their start and end apart: 1 -> 0, of which waited for: 1 -> 0; matrix products, arithmetic and copies ran while one was open for 0% -> 0% of each run, Pallas kernels for 0% -> 0%
where the time goes in v3:
time: 150 us; the launch traced here: 148 us
  Pallas kernels  144 us (96%)
  local copies, waits for them, and re-layouts  3.65 us (2%)
    pallas_call x1, Pallas kernels, on_device(): pl.pallas_call(step_kernel, out_shape=jax.ShapeDtypeStruct((256, 1024), F...  144 us

profile of v3, /device:TPU:8, one launch (start us, length us, event | category | flops | bytes accessed | tf_op | source)
XLA Modules:
  0.0 148.0 jit_solution(3804313463168982377)
XLA Ops:
  0.0 0.0 copy-start
  0.0 0.7 copy-done
  0.7 0.7 reshape.11.occ_ref
  1.3 144.4 %purify.1 = f32[256,1024]{1,0:T(8,128)} custom-call(bf16[128,4096]{1,0:T(8,128)(2,1)} %task_ref.1, s32[1,128]{1,0:T(1,128)} %bitcast.2, s32[1,128]{1,0:T(1,128)} %bitcast.3, s32[8,16]{1,0:T(8,128)} %p_pattern_ref.1, f32[8,64]{1,0:T(8,128)} %reshape.11.occ_ref, s32[8,16]{1,0:T(8,128)} %pattern_ref.1), custom_call_target="tpu_custom_call" | custom-call | tf_op jit(solution)/shard_map/purify/pallas_call | solution.py:490
  145.7 2.3 %copy.8 = f32[256,1024]{1,0:T(8,128)} copy(f32[256,1024]{1,0:T(8,128)} %purify.1) | data formatting | bytes 2097152
Async XLA Ops:
  0.0 0.7 copy-start

commit v4 on v3

--- a/solution.py
+++ b/solution.py
@@ -77,6 +77,8 @@
     column = col_id + (iota((8, 512), 1) // HALF) * BLK + iota((8, 512), 1) % HALF
     first = row_id + iota((8, 512), 0) * BLK
     quarter = iota((8, 128), 1) // HALF
+    doubled = jnp.concatenate([occ_ref[r // 2 : r // 2 + 1, :] for r in range(8)], axis=0)
+    occ = jnp.where(iota((8, 128), 0) % 2 == 0, doubled, pltpu.roll(doubled, BLK, 1))
     for quad in range(16):
         summed = dot(marks, wide[pl.ds(quad, 256, stride=16), :].astype(BF16))
         for e in range(4):
@@ -93,7 +95,7 @@
                 tiles.append(tile)
             i = quad * 4 + e
             line = jnp.concatenate(tiles, axis=1) * mask
-            line = line + jnp.where(first + i == column, occ_ref[:, i : i + 1], 0.0)
+            line = line + jnp.where(first + i == column, occ[:, i : i + 1], 0.0)
             rows[i * 8 : (i + 1) * 8, :] = line
     want = iota((256, 256), 0)
     have = iota((256, 256), 1)
@@ -104,9 +106,9 @@
 
 
 def step_kernel(
-    task_ref, owner_ref, slot_ref, p_pattern_ref, occ_ref, pattern_ref, out_ref,
-    wide, packed, by_z, twin_in, by_xy, got, info, info_z, info_xy, rows, d_ref,
-    t_local, t_send, t_recv, a, b, b2, acc, keep, low, near, far, near_in, far_in, result, swapped,
+    task_ref, owner_ref, slot_ref, p_pattern_ref, occ_ref, own_ref, other_ref,
+    wide, packed, by_z, by_xy, got, info, info_z, info_xy, rows, d_ref,
+    t_local, t_send, t_recv, a, b, b2, acc, keep, low, near, far, near_in, far_in, result,
     local_sem, y_send, y_recv, z_send, z_recv, twin_send, twin_recv,
     x_send, x_recv, r_send, r_recv, swap_send, swap_recv,
 ):
@@ -128,10 +130,9 @@
     across = device(x, y, ring(z, 4, 8), core)
 
     barrier = pltpu.get_barrier_semaphore()
-    others = [device(x, ring(y, s, 4), z, 1 - core) for s in range(1, 4)]
     spot = y * 4 + x
     plane = [(spot + s) % 16 for s in range(1, 16)]
-    others += [device(at % 4, at // 4, z, core) for at in plane]
+    others = [device(at % 4, at // 4, z, c) for at in plane for c in range(2)]
     others += [twin, across] + [device(x, y, ring(z, s, 8), core) for s in (1, -1, 2, -2)]
     for other in others:
         pl.semaphore_signal(barrier, inc=1, device_id=other, device_id_type=MESH)
@@ -178,14 +179,22 @@
 
         return arrived
 
+    def over_plane_across(source, target, recv, base):
+        for index, at in enumerate([*plane, spot]):
+            to = device(at % 4, at // 4, z, 1 - core)
+            launch(source.at[at], target.at[spot], t_send.at[base + index], t_recv.at[recv], to)
+
+        def arrived():
+            remote(target, target, t_send.at[0], t_recv.at[recv], twin).wait_recv()
+
+        return arrived
+
     info_copies = []
     for index, (shift, _, _) in enumerate(UNITS[1:]):
         to = device(x, y, ring(z, shift, 8), core)
         info_copies.append(launch(info.at[0], info_z.at[index], t_send.at[index], t_recv.at[index], to))
-    to_twin = launch(packed.at[1 - core], twin_in, t_send.at[4], t_recv.at[4], twin)
     z_tasks, z_home = over_z(packed.at[core], by_z, 5, 0)
-    to_twin.wait_recv()
-    plane_b = over_plane(lambda at: twin_in.at[at], by_xy, 13, 13, 1)
+    plane_b = over_plane_across(packed.at[1 - core], by_xy, 13, 13)
     for copy in info_copies:
         copy.wait_recv()
     unit = iota((8, 128), 0)
@@ -194,15 +203,15 @@
         fits = jnp.logical_and(unit >= low_unit, unit < low_unit + size)
         merged = jnp.where(fits, info_z[index], merged)
     info[1] = merged
-    plane_i = over_plane(lambda at: info.at[1], info_xy.at[0], 14, 28, 2)
+    plane_i = over_plane(lambda at: info.at[1], info_xy.at[0], 14, 29, 1)
     for copy in z_tasks:
         copy.wait_recv()
     z_home.wait()
-    plane_a = over_plane(lambda at: by_z.at[at], got.at[0], 15, 43, 3)
+    plane_a = over_plane(lambda at: by_z.at[at], got.at[0], 15, 44, 2)
     plane_b()
-    z_more, z_more_home = over_z(by_xy, got.at[1], 9, 4)
+    z_more, z_more_home = over_z(by_xy, got.at[1], 9, 3)
     plane_i()
-    twin_info = launch(info_xy.at[0], info_xy.at[1], t_send.at[58], t_recv.at[16], twin)
+    twin_info = launch(info_xy.at[0], info_xy.at[1], t_send.at[59], t_recv.at[16], twin)
     plane_a()
     twin_info.wait_recv()
     for copy in z_more:
@@ -374,56 +383,48 @@
     for q in range(4):
         y_arrived(q)
         hand_over(q, 0)
-        if q < 2:
+        if q < 3:
             z_issue(q, 1)
-    z_arrived(0, 1)
-    z_issue(0, 2)
-    z_arrived(1, 1)
-    z_issue(1, 2)
-    z_arrived(0, 2)
-    z_issue(0, 3)
-    z_arrived(1, 2)
-    z_issue(1, 3)
+
+    def pass_on(q, step, *then):
+        z_arrived(q, step)
+        if then:
+            z_issue(*then)
+
+    pass_on(0, 1, 0, 2)
+    pass_on(1, 1, 1, 2)
+    pass_on(2, 1, 3, 1)
+    pass_on(0, 2, 0, 3)
     x_two = x_second(lambda xx, s: b.at[s, xx], 0, x_one)
-    z_arrived(0, 3)
-    z_issue(0, 4)
-    z_arrived(1, 3)
-    z_issue(2, 1)
-    z_arrived(0, 4)
-    z_issue(1, 4)
+    pass_on(1, 2, 2, 2)
+    pass_on(3, 1, 1, 3)
+    pass_on(0, 3, 0, 4)
+    pass_on(2, 2, 3, 2)
+    pass_on(1, 3, 2, 3)
+    pass_on(0, 4, 1, 4)
     for copy in x_two:
         copy.wait_recv()
     x_one[2].wait()
     square(0)
-    z_arrived(2, 1)
-    z_issue(3, 1)
-    z_arrived(1, 4)
-    z_issue(2, 2)
+    pass_on(3, 2, 3, 3)
+    pass_on(2, 3, 2, 4)
+    reduce_pass(0, 0, 0)
+    pass_on(1, 4)
     square(1)
-    reduce_pass(0, 0, 0)
-    z_arrived(3, 1)
-    z_issue(3, 2)
+    pass_on(3, 3, 3, 4)
     gather_issue(0)
     reduce_pass(0, 1, 1)
-    z_arrived(2, 2)
-    z_issue(2, 3)
+    pass_on(2, 4)
+    square(2)
+    gather_pass(0)
     gather_issue(1)
-    gather_pass(0)
-    z_arrived(3, 2)
-    z_issue(3, 3)
+    pass_on(3, 4)
+    square(3)
     gather_pass(1)
-    z_arrived(2, 3)
-    z_issue(2, 4)
+    reduce_pass(0, 2, 2)
+    reduce_pass(0, 3, 3)
     gather_end(0)
     gather_end(1)
-    z_arrived(3, 3)
-    z_issue(3, 4)
-    z_arrived(2, 4)
-    square(2)
-    z_arrived(3, 4)
-    square(3)
-    reduce_pass(0, 2, 2)
-    reduce_pass(0, 3, 3)
     for q in range(2):
         product(q, [(zz, b2.at[0, zz]) for zz in range(4)], True)
     gather_issue(2)
@@ -435,10 +436,47 @@
     gather_end(2)
     gather_end(3)
     order = [1 - layer, 3 - layer, layer, 2 + layer]
-    for k, q in enumerate(order):
-        product(q, [(4 + zz, b2.at[1, zz]) for zz in range(4)], False)
-        reduce_issue(1, k, q)
     swaps = []
+
+    def start(k):
+        product(order[k], [(4 + zz, b2.at[1, zz]) for zz in range(4)], False)
+        reduce_issue(1, k, order[k])
+
+    def finish(k):
+        q = order[k]
+        value = (3.0 * keep[q] - 2.0 * reduce_end(1, k, q)).astype(BF16)
+        if k < 2:
+            result[k] = value
+            swaps.append(launch(result.at[k], other_ref.at[k], swap_send.at[k], swap_recv.at[k], across))
+        else:
+            own_ref[k - 2] = value
+
+    start(0)
+    start(1)
+    reduce_pass(1, 0, order[0])
+    start(2)
+    reduce_pass(1, 1, order[1])
+    finish(0)
+    start(3)
+    reduce_pass(1, 2, order[2])
+    finish(1)
+    reduce_pass(1, 3, order[3])
+    finish(2)
+    finish(3)
+    for copy in swaps:
+        copy.wait_recv()
+
+    for mine, copy in y_copies:
+        @pl.when(jnp.logical_not(mine))
+        def _():
+            copy.wait_send()
+
+    for copy in sent:
+        copy.wait_send()
+
+
+def place_kernel(own_ref, other_ref, pattern_ref, out_ref):
+    layer = lax.axis_index("layer")
     spread = (iota((16, 1024), 0) == iota((16, 1024), 1) // BLK).astype(F32)
     mask_all = dot(pattern_ref[...].astype(F32), spread)
     mask = jnp.where(layer == 0, mask_all[0:4], mask_all[4:8])
@@ -447,17 +485,9 @@
     side = jnp.where(source < 128, layer, 1 - layer)
     goes = ((source % 128) // HALF) * BLK + side * HALF + source % HALF
     place = (goes == want).astype(BF16)
-
-    def finish(k):
-        q = order[k]
-        result[k] = (3.0 * keep[q] - 2.0 * reduce_end(1, k, q)).astype(BF16)
-        if k < 2:
-            swaps.append(launch(result.at[k], swapped.at[k], swap_send.at[k], swap_recv.at[k], across))
-            return
-        half = k - 2
-        swaps[half].wait_recv()
-        own = result[k].reshape(128, 512)
-        other = swapped[half].reshape(128, 512)
+    for half in range(2):
+        own = own_ref[half].reshape(128, 512)
+        other = other_ref[half].reshape(128, 512)
         for t in range(4):
             both = jnp.concatenate([own[:, t * 128 : (t + 1) * 128], other[:, t * 128 : (t + 1) * 128]], axis=1)
             full = dot(both, place)
@@ -466,20 +496,6 @@
                     full[blk * HALF : (blk + 1) * HALF] * mask[blk : blk + 1, t * 256 : (t + 1) * 256]
                 )
 
-    for k, q in enumerate(order):
-        reduce_pass(1, k, q)
-        if k >= 1:
-            finish(k - 1)
-    finish(3)
-
-    for mine, copy in y_copies:
-        @pl.when(jnp.logical_not(mine))
-        def _():
-            copy.wait_send()
-
-    for copy in sent:
-        copy.wait_send()
-
 
 VMEM = pl.BlockSpec(memory_space=pltpu.VMEM)
 
@@ -487,15 +503,14 @@
 def on_device(tasks, task_owner, task_slot, p_pattern, c_pattern, occupations):
     dma = pltpu.SemaphoreType.DMA
     count = tasks.shape[0]
-    return pl.pallas_call(
+    own, other = pl.pallas_call(
         step_kernel,
-        out_shape=jax.ShapeDtypeStruct((256, 1024), F32),
-        in_specs=[VMEM] * 6,
-        out_specs=VMEM,
+        out_shape=[jax.ShapeDtypeStruct((2, 2, 64, 512), BF16)] * 2,
+        in_specs=[VMEM] * 5,
+        out_specs=[VMEM] * 2,
         scratch_shapes=[
             pltpu.VMEM((4096, 128), F32),
             pltpu.VMEM((2, 16, 8, 16, 128), BF16),
-            pltpu.VMEM((16, 8, 16, 128), BF16),
             pltpu.VMEM((16, 8, 16, 128), BF16),
             pltpu.VMEM((16, 8, 16, 128), BF16),
             pltpu.VMEM((2, 16, 8, 16, 128), BF16),
@@ -504,8 +519,8 @@
             pltpu.VMEM((2, 16, 8, 128), F32),
             pltpu.VMEM((512, 512), F32),
             pltpu.VMEM((2, 2, 2, 64, 512), BF16),
-            dma((5,)),
-            dma((59,)),
+            dma((4,)),
+            dma((60,)),
             dma((17,)),
             pltpu.VMEM((8, 4, 4, 2, 64, 256), BF16),
             pltpu.VMEM((2, 4, 2, 2, 64, 512), BF16),
@@ -517,7 +532,6 @@
             pltpu.VMEM((2, 4, 2, 64, 512), BF16),
             pltpu.VMEM((2, 4, 2, 2, 64, 512), BF16),
             pltpu.VMEM((2, 4, 2, 64, 512), BF16),
-            pltpu.VMEM((4, 2, 64, 512), BF16),
             pltpu.VMEM((2, 2, 64, 512), BF16),
             dma((9,)),
             dma((16,)),
@@ -539,8 +553,16 @@
         name="purify",
     )(
         tasks, task_owner.reshape(1, count), task_slot.reshape(1, count), p_pattern,
-        occupations.reshape(8, BLK), c_pattern,
+        occupations.reshape(4, 2 * BLK),
     )
+    return pl.pallas_call(
+        place_kernel,
+        out_shape=jax.ShapeDtypeStruct((256, 1024), F32),
+        in_specs=[VMEM] * 3,
+        out_specs=VMEM,
+        compiler_params=pltpu.CompilerParams(vmem_limit_bytes=16 << 20),
+        name="place",
+    )(own, other, c_pattern)
 
 
 def solution(mesh):

time: 150 us -> 135 us (0.900); the launches traced: 148 us -> 135 us
  Pallas kernels: 144 us -> 133 us
  local copies, waits for them, and re-layouts: 3.65 us -> 1.9 us
    pallas_call x1 -> x2, Pallas kernels: 144 us -> 133 us  [the longest x1 131 us: on_device(): pl.pallas_call(step_kernel, out_shape=[jax.ShapeDtypeStruct((2, 2, 64, 51...]
where the time goes in v4:
time: 135 us
  Pallas kernels  133 us (99%)
  local copies, waits for them, and re-layouts  1.9 us (1%)
    pallas_call x1, Pallas kernels, on_device(): pl.pallas_call(step_kernel, out_shape=[jax.ShapeDtypeStruct((2, 2, 64, 51...  131 us

profile of v4, /device:TPU:8, one launch (start us, length us, event | category | flops | bytes accessed | tf_op | source)
XLA Modules:
  0.0 134.7 jit_solution(9758796522707479616)
XLA Ops:
  0.0 0.0 copy-start.2
  0.0 131.4 %purify.1 = (bf16[2,2,64,512]{3,2,1,0:T(8,128)(2,1)}, bf16[2,2,64,512]{3,2,1,0:T(8,128)(2,1)}) custom-call(bf16[128,4096]{1,0:T(8,128)(2,1)} %task_ref.1, s32[1,128]{1,0:T(1,128)} %bitcast.4, s32[1,128]{1,0:T(1,128)} %bitcast.5, s32[8,16]{1,0:T(8,128)} %p_pattern_ref.1, f32[4,128]{1,0:T(4,128)} %bitcast.3), custom_call_target="tpu_custom_call" | custom-call | tf_op jit(solution)/shard_map/purify/pallas_call | solution.py:506
  131.5 0.0 copy-done.2
  131.5 0.0 copy-start
  131.5 0.9 copy-done
  132.4 0.0 copy-start.1
  132.4 0.9 copy-done.1
  133.4 1.3 place.1
Async XLA Ops:
  0.0 131.5 %copy-start.2 = (s32[8,16]{1,0:T(8,128)S(1)}, s32[8,16]{1,0:T(8,128)}, u32[]{:S(2)}) copy-start(s32[8,16]{1,0:T(8,128)} %pattern_ref.1) | copy-start | bytes 1540
  131.5 1.0 copy-start
  132.4 0.9 copy-start.1

commit v5 on v4

--- a/solution.py
+++ b/solution.py
@@ -22,25 +22,20 @@
     return jnp.dot(a, b, preferred_element_type=F32)
 
 
-UNITS = ((0, 0, 2), (1, 2, 2), (-1, 4, 2), (2, 6, 1), (-2, 7, 1))
-
-
-def z_shift(unit):
-    near_by = jnp.where(unit < 2, 0, jnp.where(unit < 4, 1, -1))
-    return jnp.where(unit == 6, 2, jnp.where(unit == 7, -2, near_by))
-
-
-def pack(task_ref, owner_ref, slot_ref, z, wide, packed, info):
+def pack(task_ref, owner_ref, slot_ref, z, core, wide, packed, info):
     count = task_ref.shape[0]
     owner = owner_ref[...]
     column = jnp.transpose(jnp.broadcast_to(owner.astype(F32), (count, count))).astype(jnp.int32)
     earlier = iota((count, count), 0) < iota((count, count), 1)
     placed = jnp.sum(jnp.logical_and(column == owner, earlier).astype(jnp.int32), axis=0, keepdims=True)
     line = iota((256, count), 0)
-    unit = line % 8
-    there = (z + z_shift(unit) + 8) % 8
-    wanted = (((line // 8) % 4) * 4 + (line // 32) % 4) * 8 + (there % 4) * 2 + line // 128
-    put = jnp.logical_and(owner == wanted, placed == unit % 2)
+    group = (line // 2) % 4
+    to_core = line // 128
+    shift = jnp.where(group == 0, 0, jnp.where(group == 1, 1, -1))
+    shift = jnp.where(group == 3, jnp.where(to_core == core, 2, -2), shift)
+    there = (z + shift + 8) % 8
+    wanted = (((line // 8) % 4) * 4 + (line // 32) % 4) * 8 + (there % 4) * 2 + to_core
+    put = jnp.logical_and(owner == wanted, placed == line % 2)
     halves = jnp.concatenate(
         [jnp.logical_and(put, there // 4 == h).astype(F32) for h in range(2)], axis=1
     ).astype(BF16)
@@ -48,13 +43,15 @@
     goes = iota((256, 256), 1)
     source = ((goes % 128) // HALF) * BLK + (goes // 128) * HALF + goes % HALF
     pick = (lane == source).astype(BF16)
-    for p in range(16):
-        piece = dot(task_ref[:, p * 256 : (p + 1) * 256], pick).astype(BF16)
-        both = jnp.concatenate([piece[:, :128], piece[:, 128:]], axis=0)
-        wide[pl.ds(p, 256, stride=16), :] = dot(halves, both)
-    for part in range(16):
-        value = wide[part * 256 : (part + 1) * 256, :].astype(BF16)
-        packed[part // 8, (part % 8) * 2 : (part % 8) * 2 + 2] = value.reshape(2, 8, 16, 128)
+    for half in range(2):
+        for quad in range(8):
+            p = half * 8 + quad
+            piece = dot(task_ref[:, p * 256 : (p + 1) * 256], pick).astype(BF16)
+            both = jnp.concatenate([piece[:, :128], piece[:, 128:]], axis=0)
+            wide[half, pl.ds(quad, 256, stride=8), :] = dot(halves, both)
+        for to in range(2):
+            value = wide[half, to * 1024 : (to + 1) * 1024, :].astype(BF16)
+            packed[half, to] = value.reshape(16, 4, 16, 128)
     slot = slot_ref[...]
     order = (slot % 16) * 8 + slot // 16 + 1
     mark = jnp.sum(jnp.where(put, order, 0).astype(F32), axis=1, keepdims=True)
@@ -63,15 +60,15 @@
     info[0] = dot(rows, jnp.where(at, mark, 0.0).astype(BF16)) - 1.0
 
 
-def assemble(got, info, lane, row_id, col_id, pattern_ref, occ_ref, wide, rows, out_ref):
-    tiles = [info[k].reshape(128, 128) for k in range(2)]
-    tiles = jnp.concatenate(tiles, axis=0)
+def find_slots(info, lane, marks):
+    tiles = jnp.concatenate([info[k].reshape(128, 128) for k in range(2)], axis=0)
     slot = jnp.sum(jnp.where(iota((256, 128), 1) == lane, tiles, 0.0), axis=1, keepdims=True)
-    marks = jnp.where(slot == iota((256, 128), 1).astype(F32), 1.0, 0.0)
-    marks = jnp.transpose(marks).astype(BF16)
-    for part in range(16):
-        value = got[part // 8, (part % 8) * 2 : (part % 8) * 2 + 2]
-        wide[part * 256 : (part + 1) * 256, :] = value.reshape(256, 128).astype(F32)
+    marks[...] = jnp.transpose(jnp.where(slot == iota((256, 128), 1).astype(F32), 1.0, 0.0)).astype(BF16)
+
+
+def assemble(half, got, marks, row_id, col_id, pattern_ref, occ_ref, wide, rows, out_ref):
+    for k in range(2):
+        wide[half, k * 1024 : (k + 1) * 1024, :] = got[half, k].reshape(1024, 128).astype(F32)
     spread = (iota((16, 512), 0) == iota((16, 512), 1) // HALF).astype(F32)
     mask = dot(pattern_ref[...].astype(F32), spread)
     column = col_id + (iota((8, 512), 1) // HALF) * BLK + iota((8, 512), 1) % HALF
@@ -79,8 +76,8 @@
     quarter = iota((8, 128), 1) // HALF
     doubled = jnp.concatenate([occ_ref[r // 2 : r // 2 + 1, :] for r in range(8)], axis=0)
     occ = jnp.where(iota((8, 128), 0) % 2 == 0, doubled, pltpu.roll(doubled, BLK, 1))
-    for quad in range(16):
-        summed = dot(marks, wide[pl.ds(quad, 256, stride=16), :].astype(BF16))
+    for quad in range(8):
+        summed = dot(marks[...], wide[half, pl.ds(quad, 256, stride=8), :].astype(BF16))
         for e in range(4):
             tiles = []
             for t in range(4):
@@ -94,19 +91,19 @@
                     tile = value if tile is None else jnp.where(quarter == f, value, tile)
                 tiles.append(tile)
             i = quad * 4 + e
+            full = half * HALF + i
             line = jnp.concatenate(tiles, axis=1) * mask
-            line = line + jnp.where(first + i == column, occ[:, i : i + 1], 0.0)
-            rows[i * 8 : (i + 1) * 8, :] = line
+            line = line + jnp.where(first + full == column, occ[:, full : full + 1], 0.0)
+            rows[half, i * 8 : (i + 1) * 8, :] = line
     want = iota((256, 256), 0)
     have = iota((256, 256), 1)
     move = (have == (want % HALF) * 8 + want // HALF).astype(BF16)
-    for h in range(2):
-        moved = dot(move, rows[h * 256 : (h + 1) * 256, :].astype(BF16)).astype(BF16)
-        out_ref[h] = moved.reshape(2, 2, 64, 512)
+    out_ref[half] = dot(move, rows[half].astype(BF16)).astype(BF16).reshape(2, 2, 64, 512)
 
 
 def step_kernel(
-    task_ref, owner_ref, slot_ref, p_pattern_ref, occ_ref, own_ref, other_ref,
+    task_hbm, owner_hbm, slot_hbm, p_pattern_hbm, occ_hbm, own_ref, other_ref,
+    task_ref, owner_ref, slot_ref, p_pattern_ref, occ_ref, load_sem, marks,
     wide, packed, by_z, by_xy, got, info, info_z, info_xy, rows, d_ref,
     t_local, t_send, t_recv, a, b, b2, acc, keep, low, near, far, near_in, far_in, result,
     local_sem, y_send, y_recv, z_send, z_recv, twin_send, twin_recv,
@@ -136,7 +133,18 @@
     others += [twin, across] + [device(x, y, ring(z, s, 8), core) for s in (1, -1, 2, -2)]
     for other in others:
         pl.semaphore_signal(barrier, inc=1, device_id=other, device_id_type=MESH)
-    pack(task_ref, owner_ref, slot_ref, z, wide, packed, info)
+    loads = [
+        pltpu.make_async_copy(src, dst, load_sem.at[index])
+        for index, (src, dst) in enumerate((
+            (owner_hbm, owner_ref), (slot_hbm, slot_ref), (task_hbm, task_ref),
+            (p_pattern_hbm, p_pattern_ref), (occ_hbm, occ_ref),
+        ))
+    ]
+    for load in loads:
+        load.start()
+    for load in loads:
+        load.wait()
+    pack(task_ref, owner_ref, slot_ref, z, core, wide, packed, info)
     pl.semaphore_wait(barrier, len(others))
 
     sent = []
@@ -157,14 +165,22 @@
         copy.start()
         return copy
 
-    def over_z(source, target, base, own):
+    def over_z(source, target, far_shift, base, own):
         copies = []
-        for index, (shift, low_unit, size) in enumerate(UNITS[1:]):
-            units = pl.ds(low_unit, size)
+        for index, shift in enumerate((1, -1, far_shift)):
             to = device(x, y, ring(z, shift, 8), core)
             at = base + index
-            copies.append(launch(source.at[:, units], target.at[:, units], t_send.at[at], t_recv.at[at], to))
-        return copies, home(source.at[:, pl.ds(0, 2)], target.at[:, pl.ds(0, 2)], own)
+            copies.append(
+                launch(source.at[:, index + 1], target.at[:, index + 1], t_send.at[at], t_recv.at[at], to)
+            )
+        copy = home(source.at[:, 0], target.at[:, 0], own)
+
+        def arrived():
+            for c in copies:
+                c.wait_recv()
+            copy.wait()
+
+        return arrived
 
     def over_plane(source, target, recv, base, own):
         for index, at in enumerate(plane):
@@ -190,40 +206,48 @@
         return arrived
 
     info_copies = []
-    for index, (shift, _, _) in enumerate(UNITS[1:]):
+    for index, shift in enumerate((1, -1, 2)):
         to = device(x, y, ring(z, shift, 8), core)
         info_copies.append(launch(info.at[0], info_z.at[index], t_send.at[index], t_recv.at[index], to))
-    z_tasks, z_home = over_z(packed.at[core], by_z, 5, 0)
-    plane_b = over_plane_across(packed.at[1 - core], by_xy, 13, 13)
+    z_tasks, plane_b = [], []
+    for half in range(2):
+        z_tasks.append(over_z(packed.at[half, core], by_z.at[half], 2, 3 + 6 * half, half))
+        plane_b.append(
+            over_plane_across(packed.at[half, 1 - core], by_xy.at[half], 15 + half, 32 + 32 * half)
+        )
     for copy in info_copies:
         copy.wait_recv()
-    unit = iota((8, 128), 0)
+    group = iota((8, 128), 0) // 2
     merged = info[0]
-    for index, (_, low_unit, size) in enumerate(UNITS[1:]):
-        fits = jnp.logical_and(unit >= low_unit, unit < low_unit + size)
-        merged = jnp.where(fits, info_z[index], merged)
+    for index in range(3):
+        merged = jnp.where(group == index + 1, info_z[index], merged)
     info[1] = merged
-    plane_i = over_plane(lambda at: info.at[1], info_xy.at[0], 14, 29, 1)
-    for copy in z_tasks:
-        copy.wait_recv()
-    z_home.wait()
-    plane_a = over_plane(lambda at: by_z.at[at], got.at[0], 15, 44, 2)
-    plane_b()
-    z_more, z_more_home = over_z(by_xy, got.at[1], 9, 3)
+    plane_i = over_plane(lambda at: info.at[1], info_xy.at[0], 17, 96, 2)
+    plane_a, z_more = [], []
+    for half in range(2):
+        z_tasks[half]()
+        plane_a.append(
+            over_plane(lambda at: by_z.at[half, at], got.at[half, 0], 18 + half, 112 + 16 * half, 3 + half)
+        )
+        plane_b[half]()
+        z_more.append(over_z(by_xy.at[half], got.at[half, 1], -2, 6 + 6 * half, 5 + half))
     plane_i()
-    twin_info = launch(info_xy.at[0], info_xy.at[1], t_send.at[59], t_recv.at[16], twin)
-    plane_a()
-    twin_info.wait_recv()
-    for copy in z_more:
-        copy.wait_recv()
-    z_more_home.wait()
-    assemble(
-        got, info_xy, core * 16 + spot, row * 512, col * 1024 + layer * HALF,
-        p_pattern_ref, occ_ref, wide, rows, d_ref,
-    )
+    twin_info = launch(info_xy.at[0], info_xy.at[1], t_send.at[144], t_recv.at[20], twin)
+
+    def tasks_arrived(half):
+        plane_a[half]()
+        z_more[half]()
+        if half == 0:
+            twin_info.wait_recv()
+            find_slots(info_xy, core * 16 + spot, marks)
+        assemble(
+            half, got, marks, row * 512, col * 1024 + layer * HALF,
+            p_pattern_ref, occ_ref, wide, rows, d_ref,
+        )
 
     y_copies = []
-    for q in range(4):
+
+    def y_issue(q):
         for p in range(2):
             for c in range(2):
                 to_y = 2 * core + p
@@ -250,8 +274,6 @@
         home = pltpu.make_async_copy(source, mine, local_sem.at[home_sem])
         home.start()
         return up, down, home
-
-    x_one = x_first(d_ref, lambda xx: b.at[:, xx], 0, 4)
 
     def x_second(pieces, sems, first):
         first[0].wait_recv()
@@ -380,6 +402,14 @@
         product(q, [(zz, b.at[zz // 4, zz % 4]) for zz in range(8)], True)
         reduce_issue(0, q, q)
 
+    tasks_arrived(0)
+    y_issue(0)
+    y_issue(1)
+    b_rows = [x_first(d_ref.at[0], lambda xx: b.at[0, xx], 20, 4)]
+    tasks_arrived(1)
+    y_issue(2)
+    y_issue(3)
+    b_rows.append(x_first(d_ref.at[1], lambda xx: b.at[1, xx], 22, 9))
     for q in range(4):
         y_arrived(q)
         hand_over(q, 0)
@@ -395,16 +425,22 @@
     pass_on(1, 1, 1, 2)
     pass_on(2, 1, 3, 1)
     pass_on(0, 2, 0, 3)
-    x_two = x_second(lambda xx, s: b.at[s, xx], 0, x_one)
+    b_rows[0][0].wait_recv()
+    below = b.at[0, ring(x, -1, 4)]
+    b_far = [launch(below, below, x_send.at[0], x_recv.at[0], up_x)]
+    b_rows[1][1].wait_recv()
+    above = b.at[1, ring(x, 1, 4)]
+    b_far.append(launch(above, above, x_send.at[1], x_recv.at[1], down_x))
     pass_on(1, 2, 2, 2)
     pass_on(3, 1, 1, 3)
     pass_on(0, 3, 0, 4)
     pass_on(2, 2, 3, 2)
     pass_on(1, 3, 2, 3)
     pass_on(0, 4, 1, 4)
-    for copy in x_two:
+    for copy in (b_rows[0][1], b_rows[1][0], *b_far):
         copy.wait_recv()
-    x_one[2].wait()
+    for copies in b_rows:
+        copies[2].wait()
     square(0)
     pass_on(3, 2, 3, 3)
     pass_on(2, 3, 2, 4)
@@ -506,22 +542,29 @@
     own, other = pl.pallas_call(
         step_kernel,
         out_shape=[jax.ShapeDtypeStruct((2, 2, 64, 512), BF16)] * 2,
-        in_specs=[VMEM] * 5,
+        in_specs=[pl.BlockSpec(memory_space=pl.ANY)] * 5,
         out_specs=[VMEM] * 2,
         scratch_shapes=[
-            pltpu.VMEM((4096, 128), F32),
-            pltpu.VMEM((2, 16, 8, 16, 128), BF16),
-            pltpu.VMEM((16, 8, 16, 128), BF16),
-            pltpu.VMEM((16, 8, 16, 128), BF16),
-            pltpu.VMEM((2, 16, 8, 16, 128), BF16),
+            pltpu.VMEM(tasks.shape, BF16),
+            pltpu.VMEM((1, count), jnp.int32),
+            pltpu.VMEM((1, count), jnp.int32),
+            pltpu.VMEM(p_pattern.shape, jnp.int32),
+            pltpu.VMEM((4, 2 * BLK), F32),
+            dma((5,)),
+            pltpu.VMEM((128, 256), BF16),
+            pltpu.VMEM((2, 2048, 128), F32),
+            pltpu.VMEM((2, 2, 16, 4, 16, 128), BF16),
+            pltpu.VMEM((2, 16, 4, 16, 128), BF16),
+            pltpu.VMEM((2, 16, 4, 16, 128), BF16),
+            pltpu.VMEM((2, 2, 16, 4, 16, 128), BF16),
             pltpu.VMEM((2, 8, 128), F32),
-            pltpu.VMEM((4, 8, 128), F32),
+            pltpu.VMEM((3, 8, 128), F32),
             pltpu.VMEM((2, 16, 8, 128), F32),
-            pltpu.VMEM((512, 512), F32),
+            pltpu.VMEM((2, 256, 512), F32),
             pltpu.VMEM((2, 2, 2, 64, 512), BF16),
-            dma((4,)),
-            dma((60,)),
-            dma((17,)),
+            dma((7,)),
+            dma((145,)),
+            dma((21,)),
             pltpu.VMEM((8, 4, 4, 2, 64, 256), BF16),
             pltpu.VMEM((2, 4, 2, 2, 64, 512), BF16),
             pltpu.VMEM((2, 4, 2, 2, 64, 512), BF16),
@@ -533,15 +576,15 @@
             pltpu.VMEM((2, 4, 2, 2, 64, 512), BF16),
             pltpu.VMEM((2, 4, 2, 64, 512), BF16),
             pltpu.VMEM((2, 2, 64, 512), BF16),
-            dma((9,)),
+            dma((10,)),
             dma((16,)),
             dma((4, 4)),
             dma((32,)),
             dma((32,)),
             dma((36,)),
             dma((36,)),
-            dma((20,)),
-            dma((20,)),
+            dma((24,)),
+            dma((24,)),
             dma((48,)),
             dma((48,)),
             dma((2,)),

time: 135 us -> 132 us (0.978)
  Pallas kernels: 133 us -> 130 us
    pallas_call x1, Pallas kernels: 131 us -> 129 us  [on_device(): pl.pallas_call(step_kernel, out_shape=[jax.ShapeDtypeStruct((2, 2, 64, 51...]
where the time goes in v5:
time: 132 us
  Pallas kernels  130 us (98%)
  local copies, waits for them, and re-layouts  1.9 us (1%)
    pallas_call x1, Pallas kernels, on_device(): pl.pallas_call(step_kernel, out_shape=[jax.ShapeDtypeStruct((2, 2, 64, 51...  129 us

profile of v5, /device:TPU:8, one launch (start us, length us, event | category | flops | bytes accessed | tf_op | source)
XLA Modules:
  0.0 132.0 jit_solution(14028394918933956412)
XLA Ops:
  0.0 0.0 copy-start.2
  0.0 128.7 %purify.1 = (bf16[2,2,64,512]{3,2,1,0:T(8,128)(2,1)}, bf16[2,2,64,512]{3,2,1,0:T(8,128)(2,1)}) custom-call(bf16[128,4096]{1,0:T(8,128)(2,1)} %task_hbm.1, s32[1,128]{1,0:T(1,128)} %bitcast.4, s32[1,128]{1,0:T(1,128)} %bitcast.5, s32[8,16]{1,0:T(8,128)} %p_pattern_hbm.1, f32[4,128]{1,0:T(4,128)} %bitcast.3), custom_call_target="tpu_custom_call" | custom-call | tf_op jit(solution)/shard_map/purify/pallas_call | solution.py:542
  128.7 0.0 copy-done.2
  128.8 0.0 copy-start
  128.8 0.9 copy-done
  129.7 0.0 copy-start.1
  129.7 0.9 copy-done.1
  130.7 1.3 place.1
Async XLA Ops:
  0.0 128.7 %copy-start.2 = (s32[8,16]{1,0:T(8,128)S(1)}, s32[8,16]{1,0:T(8,128)}, u32[]{:S(2)}) copy-start(s32[8,16]{1,0:T(8,128)} %pattern_ref.1) | copy-start | bytes 1540
  128.8 1.0 copy-start
  129.7 0.9 copy-start.1

commit v6 on v5

--- a/solution.py
+++ b/solution.py
@@ -275,15 +275,6 @@
         home.start()
         return up, down, home
 
-    def x_second(pieces, sems, first):
-        first[0].wait_recv()
-        ref = pieces(ring(x, -1, 4), 0)
-        up = launch(ref, ref, x_send.at[sems + 2], x_recv.at[sems + 2], up_x)
-        first[1].wait_recv()
-        ref = pieces(ring(x, 1, 4), 1)
-        down = launch(ref, ref, x_send.at[sems + 3], x_recv.at[sems + 3], down_x)
-        return up, down
-
     def y_arrived(q):
         for source_y in range(4):
             mine = jnp.logical_and(y == source_y, core == y // 2)
@@ -382,14 +373,31 @@
         value = reduce_end(0, q, q)
         keep[q] = value
         low[q] = value.astype(BF16)
-        x_copies[q] = x_first(low.at[q], lambda xx: b2.at[q // 2, xx, q % 2], 4 + 4 * q, 5 + q)
+        sems = 4 + 6 * q
+        here = pltpu.make_async_copy(low.at[q], b2.at[q // 2, x, q % 2], local_sem.at[5 + q])
+        here.start()
+        copies = [None] * 4
+        for part in range(2):
+            for side, to in ((0, up_x), (1, down_x)):
+                half = part if side == 0 else 1 - part
+                at = sems + 2 * part + side
+                copies[2 * part + side] = launch(
+                    low.at[q, half], b2.at[q // 2, x, q % 2, half], x_send.at[at], x_recv.at[at], to
+                )
+        x_copies[q] = (here, copies)
 
     def gather_pass(q):
-        x_copies[q] += x_second(lambda xx, s: b2.at[q // 2, xx, q % 2, s], 4 + 4 * q, x_copies[q])
+        copies = x_copies[q][1]
+        for side, to, source in ((0, up_x, ring(x, -1, 4)), (1, down_x, ring(x, 1, 4))):
+            copies[side].wait_recv()
+            ref = b2.at[q // 2, source, q % 2, side]
+            at = 4 + 6 * q + 4 + side
+            copies.append(launch(ref, ref, x_send.at[at], x_recv.at[at], to))
 
     def gather_end(q):
-        x_copies[q][2].wait()
-        for copy in x_copies[q][3:]:
+        here, copies = x_copies[q]
+        here.wait()
+        for copy in copies[2:]:
             copy.wait_recv()
 
     def all_arrived(q):
@@ -405,11 +413,11 @@
     tasks_arrived(0)
     y_issue(0)
     y_issue(1)
-    b_rows = [x_first(d_ref.at[0], lambda xx: b.at[0, xx], 20, 4)]
+    b_rows = [x_first(d_ref.at[0], lambda xx: b.at[0, xx], 28, 4)]
     tasks_arrived(1)
     y_issue(2)
     y_issue(3)
-    b_rows.append(x_first(d_ref.at[1], lambda xx: b.at[1, xx], 22, 9))
+    b_rows.append(x_first(d_ref.at[1], lambda xx: b.at[1, xx], 30, 9))
     for q in range(4):
         y_arrived(q)
         hand_over(q, 0)
@@ -511,8 +519,18 @@
         copy.wait_send()
 
 
-def place_kernel(own_ref, other_ref, pattern_ref, out_ref):
+def place_kernel(own_hbm, other_hbm, pattern_hbm, out_hbm, own_ref, other_ref, pattern_ref, out_ref, load_sem, store_sem):
     layer = lax.axis_index("layer")
+    loads = [
+        pltpu.make_async_copy(src, dst, load_sem.at[index])
+        for index, (src, dst) in enumerate(
+            ((pattern_hbm, pattern_ref), (own_hbm, own_ref), (other_hbm, other_ref))
+        )
+    ]
+    for load in loads:
+        load.start()
+    for load in loads:
+        load.wait()
     spread = (iota((16, 1024), 0) == iota((16, 1024), 1) // BLK).astype(F32)
     mask_all = dot(pattern_ref[...].astype(F32), spread)
     mask = jnp.where(layer == 0, mask_all[0:4], mask_all[4:8])
@@ -521,16 +539,23 @@
     side = jnp.where(source < 128, layer, 1 - layer)
     goes = ((source % 128) // HALF) * BLK + side * HALF + source % HALF
     place = (goes == want).astype(BF16)
-    for half in range(2):
-        own = own_ref[half].reshape(128, 512)
-        other = other_ref[half].reshape(128, 512)
-        for t in range(4):
+    stores = []
+    for t in range(4):
+        for half in range(2):
+            own = own_ref[half].reshape(128, 512)
+            other = other_ref[half].reshape(128, 512)
             both = jnp.concatenate([own[:, t * 128 : (t + 1) * 128], other[:, t * 128 : (t + 1) * 128]], axis=1)
             full = dot(both, place)
             for blk in range(4):
                 out_ref[blk * BLK + half * HALF : blk * BLK + (half + 1) * HALF, t * 256 : (t + 1) * 256] = (
                     full[blk * HALF : (blk + 1) * HALF] * mask[blk : blk + 1, t * 256 : (t + 1) * 256]
                 )
+        span = pl.ds(t * 256, 256)
+        store = pltpu.make_async_copy(out_ref.at[:, span], out_hbm.at[:, span], store_sem.at[t])
+        store.start()
+        stores.append(store)
+    for store in stores:
+        store.wait()
 
 
 VMEM = pl.BlockSpec(memory_space=pltpu.VMEM)
@@ -583,8 +608,8 @@
             dma((32,)),
             dma((36,)),
             dma((36,)),
-            dma((24,)),
-            dma((24,)),
+            dma((32,)),
+            dma((32,)),
             dma((48,)),
             dma((48,)),
             dma((2,)),
@@ -601,9 +626,17 @@
     return pl.pallas_call(
         place_kernel,
         out_shape=jax.ShapeDtypeStruct((256, 1024), F32),
-        in_specs=[VMEM] * 3,
-        out_specs=VMEM,
-        compiler_params=pltpu.CompilerParams(vmem_limit_bytes=16 << 20),
+        in_specs=[pl.BlockSpec(memory_space=pl.ANY)] * 3,
+        out_specs=pl.BlockSpec(memory_space=pl.ANY),
+        scratch_shapes=[
+            pltpu.VMEM((2, 2, 64, 512), BF16),
+            pltpu.VMEM((2, 2, 64, 512), BF16),
+            pltpu.VMEM(c_pattern.shape, jnp.int32),
+            pltpu.VMEM((256, 1024), F32),
+            dma((3,)),
+            dma((4,)),
+        ],
+        compiler_params=pltpu.CompilerParams(vmem_limit_bytes=56 << 20),
         name="place",
     )(own, other, c_pattern)
 

time: 132 us -> 131 us (level)
  local copies, waits for them, and re-layouts: 1.9 us -> 0 us
    unnamed x6 -> x0, local copies, waits for them, and re-layouts: 1.9 us -> none
where the time goes in v6:
time: 131 us; the launch traced here: 130 us
  Pallas kernels  130 us (99%)
    pallas_call x1, Pallas kernels, on_device(): pl.pallas_call(step_kernel, out_shape=[jax.ShapeDtypeStruct((2, 2, 64, 51...  128 us

profile of v6, /device:TPU:8, one launch (start us, length us, event | category | flops | bytes accessed | tf_op | source)
XLA Modules:
  0.0 130.5 jit_solution(13683484153738793126)
XLA Ops:
  0.0 128.2 %purify.1 = (bf16[2,2,64,512]{3,2,1,0:T(8,128)(2,1)}, bf16[2,2,64,512]{3,2,1,0:T(8,128)(2,1)}) custom-call(bf16[128,4096]{1,0:T(8,128)(2,1)} %task_hbm.1, s32[1,128]{1,0:T(1,128)} %bitcast.4, s32[1,128]{1,0:T(1,128)} %bitcast.5, s32[8,16]{1,0:T(8,128)} %p_pattern_hbm.1, f32[4,128]{1,0:T(4,128)} %bitcast.3), custom_call_target="tpu_custom_call" | custom-call | tf_op jit(solution)/shard_map/purify/pallas_call | solution.py:567
  128.2 2.3 %place.1 = f32[256,1024]{1,0:T(8,128)} custom-call(bf16[2,2,64,512]{3,2,1,0:T(8,128)(2,1)} %get-tuple-element.7.own_hbm, bf16[2,2,64,512]{3,2,1,0:T(8,128)(2,1)} %get-tuple-element.8.other_hbm, s32[8,16]{1,0:T(8,128)} %pattern_hbm.1), custom_call_target="tpu_custom_call" | custom-call | tf_op jit(solution)/shard_map/place/pallas_call | solution.py:626

commit v7 on v6

--- a/solution.py
+++ b/solution.py
@@ -500,8 +500,8 @@
     reduce_pass(1, 0, order[0])
     start(2)
     reduce_pass(1, 1, order[1])
+    start(3)
     finish(0)
-    start(3)
     reduce_pass(1, 2, order[2])
     finish(1)
     reduce_pass(1, 3, order[3])

time: 131 us -> 131 us (level)
  no operation moved by 1% of the time
where the time goes in v7:
time: 131 us; the launch traced here: 130 us
  Pallas kernels  130 us (99%)
    pallas_call x1, Pallas kernels, on_device(): pl.pallas_call(step_kernel, out_shape=[jax.ShapeDtypeStruct((2, 2, 64, 51...  128 us

profile of v7, /device:TPU:8, one launch (start us, length us, event | category | flops | bytes accessed | tf_op | source)
XLA Modules:
  0.0 130.5 jit_solution(1617775023492319213)
XLA Ops:
  0.0 128.2 %purify.1 = (bf16[2,2,64,512]{3,2,1,0:T(8,128)(2,1)}, bf16[2,2,64,512]{3,2,1,0:T(8,128)(2,1)}) custom-call(bf16[128,4096]{1,0:T(8,128)(2,1)} %task_hbm.1, s32[1,128]{1,0:T(1,128)} %bitcast.4, s32[1,128]{1,0:T(1,128)} %bitcast.5, s32[8,16]{1,0:T(8,128)} %p_pattern_hbm.1, f32[4,128]{1,0:T(4,128)} %bitcast.3), custom_call_target="tpu_custom_call" | custom-call | tf_op jit(solution)/shard_map/purify/pallas_call | solution.py:567
  128.2 2.3 %place.1 = f32[256,1024]{1,0:T(8,128)} custom-call(bf16[2,2,64,512]{3,2,1,0:T(8,128)(2,1)} %get-tuple-element.7.own_hbm, bf16[2,2,64,512]{3,2,1,0:T(8,128)(2,1)} %get-tuple-element.8.other_hbm, s32[8,16]{1,0:T(8,128)} %pattern_hbm.1), custom_call_target="tpu_custom_call" | custom-call | tf_op jit(solution)/shard_map/place/pallas_call | solution.py:626
